TPU v7x, 256 devices: a whole 4x4x8 slice. The times are simulated.
256 devices in a mesh: seq: 32 (over z, y), head: 8 (over x, core).
Axes of the slice: x: 4, y: 4, z: 8, core: 2. Of those that a mesh axis runs over, the one named last changes fastest.
Arguments:
- queries: bfloat16 [16384, 2048], P('seq', 'head'), may hold values from -6 to 6
- key_vectors: bfloat16 [16384, 2048], P('seq', 'head'), may hold values from -6 to 6
- values: bfloat16 [16384, 4096], P('seq', 'head'), may hold values from -24 to 24
- gate_log: float32 [32, 16384], P('head', 'seq'), may hold values from -1 to 0
- write_rate: float32 [32, 16384], P('head', 'seq'), as said below
- prompt_stretches: int32 [4], replicated, may hold values from 1 to 128, as said below
- decode_owner: int32 [4], replicated, may hold values from 0 to 31, as said below
- norm_gain: float32 [128], replicated, may hold values from 0.25 to 1.75
- out_weight: bfloat16 [4096, 2048], P('head'), may hold values from -0.09375 to 0.09375
Outputs:
- mixed: bfloat16 [16384, 2048], P('seq', 'head')
- decode_states: float32 [32, 32, 128, 128], P('seq', 'head')
Inputs may be any that keep to these rules, and one draw needn't show every extreme that they name: `prompt_stretches`: prompts lie in order along the token dimension, each a whole number of stretches of 64 tokens; the lengths sum to 256 and the longest is exactly 128. `decode_owner`: the 4 entries are distinct. `write_rate`: every entry is positive.
All inputs are finite; a program needn't handle non-finite values.
Results may differ from a plain program's by a relative error of at most 0.014.
Values may be sent and summed in bfloat16 or wider, within the bound.
No kernel may reach another device: no remote copies, remote signals or barrier semaphores. Data moves between devices by JAX's collectives and lax.ppermute only.
A program may use at most 64 MiB of HBM per device.

v0:
```python
import jax
import jax.numpy as jnp
from jax import lax
from jax.experimental import pallas as pl
from jax.experimental.pallas import tpu as pltpu
from jax.sharding import PartitionSpec as P


DK = 128
DV = 128
STRETCH = 64
PAIR = 2 * STRETCH
ROWS, COLS = 4, 8
F32 = jnp.float32
BF16 = jnp.bfloat16
GROUP = 4

NN = (((1,), (0,)), ((), ()))
NT = (((1,), (1,)), ((), ()))
TN = (((0,), (0,)), ((), ()))


def dot(a, b, dims=NN):
    return lax.dot_general(a, b, dims, preferred_element_type=F32)


def halves(x):
    high = x.astype(BF16)
    return high, (x - high.astype(F32)).astype(BF16)


def thirds(x):
    high = x.astype(BF16)
    rest = x - high.astype(F32)
    middle = rest.astype(BF16)
    return high, middle, (rest - middle.astype(F32)).astype(BF16)


def dot3(a, b):
    return dot_left(a, b[0]) + dot(a[0], b[1])


def dot_left(a, b):
    rows = a[0].shape[0]
    both = dot(jnp.concatenate(a, axis=0), b)
    return both[:rows] + both[rows:]


def spans(size, row, col):
    return (row // size) == (col // size)


def local_kernel(
    number,
    lengths_ref,
    position_ref,
    query_ref,
    key_ref,
    value_ref,
    gate_ref,
    rate_ref,
    out_ref,
    block_ref,
    close_ref,
    flag_ref,
    w_s,
    u_s,
    score_s,
    grow_s,
    keep_s,
    last_s,
    state_s,
    gates_s,
):
    for n in range(number):
        lanes = slice(n * STRETCH, (n + 1) * STRETCH)
        for kind, ref in enumerate((gate_ref, rate_ref)):
            for h in range(4):
                gates_s[n, 2 * kind + h // 2, 0:1, (h % 2) * STRETCH : (h % 2 + 1) * STRETCH] = ref[
                    h : h + 1, lanes
                ]

    row = lax.broadcasted_iota(jnp.int32, (PAIR, PAIR), 0)
    col = lax.broadcasted_iota(jnp.int32, (PAIR, PAIR), 1)
    same = spans(STRETCH, row, col)
    eye = row == col
    causal = same & (row >= col)
    strict = same & (row > col)
    ones_low = jnp.where(causal, 1.0, 0.0).astype(BF16)
    ones_up = jnp.where(same & (row <= col), 1.0, 0.0).astype(BF16)
    ones_all = jnp.where(same, 1.0, 0.0).astype(BF16)
    ones_eye = jnp.where(eye, 1.0, 0.0).astype(BF16)
    left = jnp.concatenate([ones_low, ones_all, ones_eye], axis=0)

    identity = jnp.where(eye, 1.0, 0.0)
    small_mask = strict & spans(8, row, col)
    edge_masks = [
        strict & spans(size, row, col) & ~spans(size // 2, row, col) for size in (16, 32, 64)
    ]

    def solve(turn, carry):
        count = 2 * GROUP
        units = [2 * turn * GROUP + i for i in range(count)]
        systems, keyed, valued, norms, rates = [], [], [], [], []
        for i in range(GROUP):
            n = turn * GROUP + i
            rows = pl.ds(pl.multiple_of(n * STRETCH, STRETCH), STRETCH)
            gates = jnp.concatenate([gates_s[n, j, 0:1, :] for j in range(4)] * 2, axis=0)
            parts = thirds(gates)
            columns = dot(left, parts[0], NT) + (
                dot(left, parts[1], NT) + dot(left, parts[2], NT)
            )
            sums = dot(parts[0], ones_up) + (dot(parts[1], ones_up) + dot(parts[2], ones_up))
            for c in range(2):
                unit = units[2 * i + c]
                lanes = slice(c * DK, (c + 1) * DK)
                keys = key_ref[rows, lanes]
                queries = query_ref[rows, lanes]
                kk = jnp.concatenate([keys, keys], axis=0)
                qq = jnp.concatenate([queries, queries], axis=0)
                vv = jnp.concatenate(
                    [
                        value_ref[rows, (2 * c + r) * DV : (2 * c + r + 1) * DV]
                        for r in range(2)
                    ],
                    axis=0,
                )
                products = dot(jnp.concatenate([kk, queries], axis=0), kk, NT)
                gram = products[:PAIR]
                cross = jnp.concatenate([products[PAIR:]] * 2, axis=0)
                diagonal = jnp.where(eye, gram, 0.0)
                norm_col = lax.rsqrt(jnp.sum(diagonal, axis=1, keepdims=True) + 1e-06)
                norm_row = lax.rsqrt(jnp.sum(diagonal, axis=0, keepdims=True) + 1e-06)
                wide = qq.astype(F32)
                norm_query = lax.rsqrt(
                    jnp.sum(wide * wide, axis=1, keepdims=True) + 1e-06
                ) * DK ** (-0.5)
                sum_col = columns[:PAIR, c : c + 1]
                last_col = columns[PAIR : 2 * PAIR, c : c + 1]
                rate_col = columns[2 * PAIR :, 2 + c : 3 + c]
                sum_row = sums[c : c + 1]
                decay = jnp.exp(jnp.where(causal, sum_col - sum_row, -1e30))
                scaled = norm_row * decay
                systems.append(
                    jnp.where(strict, gram * (rate_col * norm_col) * scaled, 0.0)
                )
                score_s[unit] = (cross * norm_query * scaled).astype(BF16)
                grow_s[unit] = jnp.broadcast_to(jnp.exp(sum_col) * norm_query, (PAIR, DK))
                keep_s[unit] = jnp.broadcast_to(
                    jnp.exp(last_col - sum_col) * norm_col, (PAIR, DK)
                )
                last_s[unit] = jnp.broadcast_to(jnp.exp(last_col), (PAIR, DK))
                keyed.append(kk)
                valued.append(vv)
                rates.append(gates[2 + c : 3 + c])
                norms.append(jnp.exp(sum_row) * norm_row)

        small = [jnp.where(small_mask, x, 0.0) for x in systems]
        small_parts = [halves(x) for x in small]
        second = [halves(dot3(x, x)) for x in small_parts]
        inverse = [identity - x for x in small]
        inverse = [x + dot3(halves(x), y) for x, y in zip(inverse, second)]
        fourth = [halves(dot3(x, x)) for x in second]
        inverse = [x + dot3(halves(x), y) for x, y in zip(inverse, fourth)]
        for mask in edge_masks:
            parts = [halves(x) for x in inverse]
            edges = [halves(jnp.where(mask, x, 0.0)) for x in systems]
            inner = [halves(dot3(x, y)) for x, y in zip(edges, parts)]
            inverse = [x - dot3(y, z) for x, y, z in zip(inverse, parts, inner)]
        for i in range(count):
            scaled = inverse[i] * rates[i]
            u_s[units[i]] = dot_left(halves(scaled), valued[i])
            high, low = halves(dot_left(halves(scaled * norms[i]), keyed[i]))
            w_s[units[i], 0] = high
            w_s[units[i], 1] = low
        return carry

    lax.fori_loop(0, number // GROUP, solve, 0)

    close_ref[...] = jnp.zeros_like(close_ref)
    finish, total = [], 0
    for p in range(4):
        total = total + lengths_ref[p]
        finish.append(total)
    row_first = (position_ref[0] // ROWS) * ROWS
    for y in range(ROWS):
        start = (row_first + y) * number
        for p in range(4):
            active = finish[p] > start
            if p > 0:
                active = active & (finish[p - 1] <= start)
            flag_ref[y, p] = jnp.broadcast_to(jnp.where(active, 1.0, 0.0), (1, DV))
    first = jnp.concatenate(
        [jnp.zeros((DK, DV), F32), jnp.where(eye, 1.0, 0.0)], axis=1
    )
    for h in range(4):
        state_s[h] = first

    def walk(n, carry):
        rows = pl.ds(pl.multiple_of(n * STRETCH, STRETCH), STRETCH)
        ident = position_ref[0] * number + n
        opening = ident == 0
        for p in range(3):
            opening = opening | (ident == finish[p])
        alive = jnp.where(opening, 0.0, 1.0)
        heads = [(c, r) for c in range(2) for r in range(2)]
        tops = [slice(r * STRETCH, (r + 1) * STRETCH) for r in range(2)]
        keys = [key_ref[rows, c * DK : (c + 1) * DK] for c in range(2)]
        queries = [query_ref[rows, c * DK : (c + 1) * DK] for c in range(2)]
        states, pulled, asked = [], [], []
        for c, r in heads:
            unit = 2 * n + c
            state = state_s[2 * c + r] * alive
            high, low = halves(state)
            w_high, w_low = w_s[unit, 0, tops[r], :], w_s[unit, 1, tops[r], :]
            first = dot(jnp.concatenate([w_high, w_low, queries[c]], axis=0), high)
            rest = dot(jnp.concatenate([w_high, queries[c]], axis=0), low)
            pulled.append(first[:STRETCH] + (first[STRETCH : 2 * STRETCH] + rest[:STRETCH]))
            asked.append(first[2 * STRETCH :] + rest[STRETCH:])
            states.append(state)
        fresh, kept = [], []
        for c in range(2):
            unit = 2 * n + c
            base = jnp.concatenate([u_s[unit], jnp.zeros((PAIR, DK), F32)], axis=1)
            keep = jnp.concatenate([keep_s[unit]] * 2, axis=1)
            fresh.append(base - jnp.concatenate(pulled[2 * c : 2 * c + 2], axis=0))
            kept.append(halves(keep * fresh[c]))
        for c, r in heads:
            h = 2 * c + r
            retain = last_s[2 * n + c, r * STRETCH : r * STRETCH + 1, :]
            retain = jnp.concatenate([retain] * 2, axis=1)
            doubled = jnp.concatenate([keys[c], keys[c]], axis=0)
            both = jnp.concatenate([kept[c][0][tops[r]], kept[c][1][tops[r]]], axis=0)
            state_s[h] = retain * states[h] + dot(doubled, both, TN)
        for c in range(2):
            unit = 2 * n + c
            grow = jnp.concatenate([grow_s[unit]] * 2, axis=1)
            high, low = halves(fresh[c])
            output = grow * jnp.concatenate(asked[2 * c : 2 * c + 2], axis=0) + (
                dot(score_s[unit], high) + dot(score_s[unit], low)
            )
            for r in range(2):
                out_ref[2 * c + r, rows, :] = output[tops[r]]

        for p in range(4):

            @pl.when(ident + 1 == finish[p])
            def _(p=p):
                for h in range(4):
                    close_ref[h, p] = state_s[h, :, :DV].astype(BF16)
                    close_ref[h, 4] = (
                        close_ref[h, 4].astype(F32) + state_s[h, :, DV:]
                    ).astype(BF16)

        return carry

    lax.fori_loop(0, number, walk, 0)
    for h in range(4):
        block_ref[h, 0] = state_s[h, :, :DV].astype(BF16)
        block_ref[h, 1] = state_s[h, :, DV:].astype(BF16)


def send_kernel(place_ref, out_ref, arriving_ref, gain_ref, weight_ref, hidden_ref, send_ref):
    gain = gain_ref[...]
    for h in range(4):
        output = out_ref[h, :, :DV] + dot_left(halves(out_ref[h, :, DV:]), arriving_ref[h])
        scale = lax.rsqrt(jnp.mean(output * output, axis=1, keepdims=True) + 1e-06)
        hidden_ref[:, h * DV : (h + 1) * DV] = (output * scale * gain).astype(BF16)
    width = send_ref.shape[2]
    place, core = place_ref[0] // 2, place_ref[0] % 2
    for k in range(4):
        j = ((place + k) % 4) * 2 + 1 - core
        columns = weight_ref[:, pl.ds(pl.multiple_of(j * width, width), width)]
        send_ref[k] = dot(hidden_ref[...], columns).astype(BF16)


def keep_kernel(place_ref, hidden_ref, weight_ref, other_ref, *kept_refs):
    width = other_ref.shape[2]
    place, core = place_ref[0] // 2, place_ref[0] % 2
    for k in range(4):
        j = ((place + k) % 4) * 2 + core
        columns = weight_ref[:, pl.ds(pl.multiple_of(j * width, width), width)]
        total = dot(hidden_ref[...], columns) + other_ref[k].astype(F32)
        kept_refs[k][...] = total.astype(BF16)


VMEM = pl.BlockSpec(memory_space=pltpu.VMEM)
SMEM = pl.BlockSpec(memory_space=pltpu.SMEM)


def shifted(block, distance):
    count = lax.axis_size("seq")
    return lax.ppermute(block, "seq", [(i, i + distance) for i in range(count - distance)])


def swapped(block, distance):
    count = lax.axis_size("seq")
    return lax.ppermute(block, "seq", [(i, i ^ distance) for i in range(count)])


def traded(blocks):
    count = lax.axis_size("seq")
    groups = [[first + y for y in range(ROWS)] for first in range(0, count, ROWS)]
    return lax.all_to_all(blocks, "seq", 0, 0, axis_index_groups=groups)


def chained(later, earlier):
    if later.ndim == 2:
        state, link = later[:, :DV], later[:, DV:]
    else:
        state, link = later[0], later[1]
    state = jnp.pad(state.astype(F32), ((0, 0), (0, DK)))
    return dot(link, earlier) + state


def program(
    queries,
    key_vectors,
    values,
    gate_log,
    write_rate,
    prompt_stretches,
    decode_owner,
    norm_gain,
    out_weight,
):
    local_rows = queries.shape[0]
    number = local_rows // STRETCH
    position = lax.axis_index("seq")
    place = lax.axis_index("head")
    here = position[None].astype(jnp.int32)

    def kernel(*refs):
        local_kernel(number, *refs)

    units = 2 * number
    out, block, closing, flags = pl.pallas_call(
        kernel,
        out_shape=(
            jax.ShapeDtypeStruct((4, local_rows, 2 * DV), F32),
            jax.ShapeDtypeStruct((4, 2, DK, DV), BF16),
            jax.ShapeDtypeStruct((4, 5, DK, DV), BF16),
            jax.ShapeDtypeStruct((ROWS, 4, 1, DV), F32),
        ),
        in_specs=[SMEM] * 2 + [VMEM] * 5,
        out_specs=(VMEM,) * 4,
        scratch_shapes=[
            pltpu.VMEM((units, 2, PAIR, DK), BF16),
            pltpu.VMEM((units, PAIR, DK), F32),
            pltpu.VMEM((units, PAIR, PAIR), BF16),
        ]
        + [pltpu.VMEM((units, PAIR, DK), F32)] * 3
        + [pltpu.VMEM((4, DK, 2 * DV), F32), pltpu.VMEM((number, 4, 8, PAIR), F32)],
        name="local",
    )(prompt_stretches, here, queries, key_vectors, values, gate_log, write_rate)

    blocks = traded(block)
    closings = traded(closing)
    both = jnp.concatenate([blocks[0, 0], blocks[0, 1]], axis=1).astype(F32)
    prefix = [both]
    for y in range(1, 4):
        both = chained(blocks[y], both.astype(BF16))
        prefix.append(both)
    before = shifted(both.astype(BF16), ROWS)
    window = chained(prefix.pop().astype(BF16), before).astype(BF16)
    near = shifted(window, ROWS)
    far = shifted(window[:, :DV], 3 * ROWS)
    entering = near[:, :DV].astype(F32) + dot(near[:, DV:], far)
    prefix = jnp.stack(prefix)
    moved = jnp.einsum(
        "yde,ef->ydf", prefix[:, :, DV:].astype(BF16), entering.astype(BF16), preferred_element_type=F32
    )
    starts = jnp.concatenate([entering[None], prefix[:, :, :DV] + moved]).astype(BF16)
    starts, closings = lax.optimization_barrier((starts, closings))
    arriving = traded(starts)

    row = position // ROWS
    moved = jnp.einsum("yde,yef->ydf", closings[:, 4], starts, preferred_element_type=F32)
    finals = sum(
        closings[y, :4].astype(F32) + flags[y] * moved[y][None] for y in range(ROWS)
    ).astype(BF16)

    width = out_weight.shape[1] // COLS
    there = place[None].astype(jnp.int32)
    hidden, outgoing = pl.pallas_call(
        send_kernel,
        out_shape=(
            jax.ShapeDtypeStruct((local_rows, 4 * DV), BF16),
            jax.ShapeDtypeStruct((4, local_rows, width), BF16),
        ),
        in_specs=[SMEM] + [VMEM] * 4,
        out_specs=(VMEM,) * 2,
        name="send",
    )(there, out, arriving, norm_gain[None, :], out_weight)
    incoming = lax.ppermute(outgoing, "head", [(i, i ^ 1) for i in range(COLS)])
    kept = pl.pallas_call(
        keep_kernel,
        out_shape=(jax.ShapeDtypeStruct((local_rows, width), BF16),) * 4,
        in_specs=[SMEM] + [VMEM] * 3,
        out_specs=(VMEM,) * 4,
        name="keep",
    )(there, hidden, out_weight, incoming)
    finals = finals + swapped(finals, ROWS)
    finals, *kept = lax.optimization_barrier((finals, *kept))
    moved = [
        lax.ppermute(kept[k], "head", [(i, (i + 2 * k) % COLS) for i in range(COLS)])
        for k in (1, 3, 2)
    ]
    for distance in (2 * ROWS, 4 * ROWS):
        finals = finals + swapped(finals, distance)
    owners = row * ROWS + jnp.arange(ROWS, dtype=jnp.int32)
    chosen = (decode_owner[None, :] == owners[:, None])[:, :, None, None]
    parcels = jnp.sum(jnp.where(chosen, finals[None].astype(F32), 0.0), axis=1).astype(BF16)
    owned = traded(parcels).astype(F32)
    mixed = kept[0].astype(F32)
    for part in moved:
        mixed = mixed + part.astype(F32)
    return (mixed.astype(BF16), owned[None])


def solution(mesh):
    return jax.shard_map(
        program,
        mesh=mesh,
        in_specs=(
            P("seq", "head"),
            P("seq", "head"),
            P("seq", "head"),
            P("head", "seq"),
            P("head", "seq"),
            P(),
            P(),
            P(),
            P("head", None),
        ),
        out_specs=(P("seq", "head"), P("seq", "head", None, None)),
        check_vma=False,
    )
```

profile of v0, /device:TPU:8, one launch (start us, length us, event | category | flops | bytes accessed | tf_op | source)
XLA Modules:
  0.0 111.4 jit_solution(4557614133981024178)
XLA Ops:
  0.6 0.0 copy-start.4
  0.6 15.3 %local.1 = (f32[4,512,256]{2,1,0:T(8,128)}, bf16[4,2,128,128]{3,2,1,0:T(8,128)(2,1)}, bf16[4,5,128,128]{3,2,1,0:T(8,128)(2,1)}, f32[4,4,1,128]{3,2,1,0:T(1,128)}) custom-call(s32[4]{0:T(128)} %refs_0_.1, s32[1]{0:T(128)} %bitcast.refs_1_, bf16[512,256]{1,0:T(8,128)(2,1)} %refs_2_.1, bf16[512,256]{1,0:T(8,128)(2,1)} %refs_3_.1, bf16[512,512]{1,0:T(8,128)(2,1)} %refs_4_.1, ...), custom_call_target="tpu_custom_call" | custom-call | tf_op jit(solution)/shard_map/local/pallas_call | solution.py:337
  15.9 10.8 %all_to_all.20 = bf16[4,2,128,128]{3,2,1,0:T(8,128)(2,1)S(1)} all-to-all(bf16[4,2,128,128]{3,2,1,0:T(8,128)(2,1)} %get-tuple-element.19), channel_id=1, replica_groups={{0,8,16,24},{32,40,48,56},{64,72,80,88},{96,104,112,120},{128,136,144,1..., dimensions={0} | all-to-all | bytes 524288 | tf_op jit(solution)/shard_map/all_to_all | solution.py:304
  26.7 0.0 copy-start.2
  26.7 5.0 %all-to-all-start.1 = ((bf16[4,5,128,128]{3,2,1,0:T(8,128)(2,1)}), bf16[4,5,128,128]{3,2,1,0:T(8,128)(2,1)S(1)}, u32[]{:S(2)}, u32[]{:S(2)}) async-start(bf16[4,5,128,128]{3,2,1,0:T(8,128)(2,1)} %get-tuple-element.20), calls=%async_computation.1 | async-start | bytes 1310720 | tf_op jit(solution)/shard_map/all_to_all | solution.py:304
  31.8 0.1 convolution_add_fusion.4
  31.9 0.1 convolution_add_fusion.3
  32.1 0.1 fusion.1
  32.2 3.2 %collective-permute-start = (bf16[128,256]{1,0:T(8,128)(2,1)S(1)}, bf16[128,256]{1,0:T(8,128)(2,1)S(1)}, u32[]{:S(2)}, u32[]{:S(2)}) collective-permute-start(bf16[128,256]{1,0:T(8,128)(2,1)S(1)} %fusion.1), channel_id=1, source_target_pairs={{0,32},{8,40},{16,48},{24,56},{32,64},{40,72},{48,80},{56,88},{64,... | collective-permute-start | bytes 196616 | tf_op jit(solution)/shard_map/ppermute | solution.py:293
  35.4 1.9 %collective-permute-done = bf16[128,256]{1,0:T(8,128)(2,1)S(1)} collective-permute-done((bf16[128,256]{1,0:T(8,128)(2,1)S(1)}, bf16[128,256]{1,0:T(8,128)(2,1)S(1)}, u32[]{:S(2)}, u32[]{:S(2)}) %collective-permute-start) | collective-permute-done | bytes 65568 | tf_op jit(solution)/shard_map/ppermute | solution.py:293
  37.3 0.0 copy-done.4
  37.3 0.1 fusion.2
  37.5 4.3 %collective-permute-start.1 = (bf16[128,256]{1,0:T(8,128)(2,1)S(1)}, bf16[128,256]{1,0:T(8,128)(2,1)S(1)}, u32[]{:S(2)}, u32[]{:S(2)}) collective-permute-start(bf16[128,256]{1,0:T(8,128)(2,1)S(1)} %fusion.2), channel_id=1, source_target_pairs={{0,32},{8,40},{16,48},{24,56},{32,64},{40,72},{48,80},{56,88},{64,... | collective-permute-start | bytes 196616 | tf_op jit(solution)/shard_map/ppermute | solution.py:293
  41.7 9.0 %collective-permute-start.2 = (bf16[128,128]{1,0:T(8,128)(2,1)S(1)}, bf16[128,128]{1,0:T(8,128)(2,1)S(1)}, u32[]{:S(2)}, u32[]{:S(2)}) collective-permute-start(bf16[128,128]{1,0:T(8,128)(2,1)S(1)} %slice.137), channel_id=1, source_target_pairs={{0,96},{8,104},{16,112},{24,120},{32,128},{40,136},{48,144},{56,15... | collective-permute-start | bytes 98312 | tf_op jit(solution)/shard_map/ppermute | solution.py:293
  50.7 1.5 %collective-permute-done.2 = bf16[128,128]{1,0:T(8,128)(2,1)S(1)} collective-permute-done((bf16[128,128]{1,0:T(8,128)(2,1)S(1)}, bf16[128,128]{1,0:T(8,128)(2,1)S(1)}, u32[]{:S(2)}, u32[]{:S(2)}) %collective-permute-start.2) | collective-permute-done | bytes 32800 | tf_op jit(solution)/shard_map/ppermute | solution.py:293
  52.3 0.0 collective-permute-done.1
  52.3 0.1 add_convert_fusion.2
  52.4 0.2 fusion
  52.6 0.7 pad_maximum_fusion.1
  53.2 0.0 all-to-all-done.1
  53.3 4.8 %all-to-all-start.2 = ((bf16[4,128,128]{2,1,0:T(8,128)(2,1)}), bf16[4,128,128]{2,1,0:T(8,128)(2,1)S(1)}, u32[]{:S(2)}, u32[]{:S(2)}) async-start(bf16[4,128,128]{2,1,0:T(8,128)(2,1)} %pad_maximum_fusion.1), calls=%async_computation.2 | async-start | bytes 262144 | tf_op jit(solution)/shard_map/all_to_all | solution.py:304
  58.0 0.0 copy-done.2
  58.1 4.5 %all-to-all-done.2.arriving_ref = bf16[4,128,128]{2,1,0:T(8,128)(2,1)S(1)} async-done(((bf16[4,128,128]{2,1,0:T(8,128)(2,1)}), bf16[4,128,128]{2,1,0:T(8,128)(2,1)S(1)}, u32[]{:S(2)}, u32[]{:S(2)}) %all-to-all-start.2) | async-done | bytes 131104 | tf_op jit(solution)/shard_map/all_to_all | solution.py:304
  62.6 0.0 copy-start.1
  62.6 0.7 copy-done.1
  63.2 4.4 %send.1 = (bf16[512,512]{1,0:T(8,128)(2,1)}, bf16[4,512,256]{2,1,0:T(8,128)(2,1)}) custom-call(s32[1]{0:T(128)} %bitcast.28.place_ref, f32[4,512,256]{2,1,0:T(8,128)} %get-tuple-element.24.out_ref, bf16[4,128,128]{2,1,0:T(8,128)(2,1)} %copy-done.1, f32[1,128]{1,0:T(1,128)} %bitcast.84, bf16[512,2048]{1,0:T(8,128)(2,1)} %weight_ref.3), custom_call_target="tpu_custom_call" | custom-call | tf_op jit(solution)/shard_map/send/pallas_call | solution.py:385
  67.6 0.0 collective-permute-start.4
  67.7 1.1 fusion.7
  68.8 0.2 fusion.4
  68.9 0.1 collective-permute-start.3
  69.0 5.9 %collective-permute-done.3 = bf16[4,128,128]{2,1,0:T(8,128)(2,1)S(1)} collective-permute-done((bf16[4,128,128]{2,1,0:T(8,128)(2,1)S(1)}, bf16[4,128,128]{2,1,0:T(8,128)(2,1)S(1)}, u32[]{:S(2)}, u32[]{:S(2)}) %collective-permute-start.3) | collective-permute-done | bytes 131104 | tf_op jit(solution)/shard_map/ppermute | solution.py:298
  74.9 0.2 fusion.26
  75.1 0.0 copy-start.3
  75.1 0.0 collective-permute-done.4.other_ref
  75.1 0.0 copy-start
  75.1 1.0 copy-done
  76.1 3.5 %keep.1 = (bf16[512,256]{1,0:T(8,128)(2,1)}, bf16[512,256]{1,0:T(8,128)(2,1)}, bf16[512,256]{1,0:T(8,128)(2,1)}, bf16[512,256]{1,0:T(8,128)(2,1)}) custom-call(s32[1]{0:T(128)} %bitcast.28.place_ref, bf16[512,512]{1,0:T(8,128)(2,1)} %get-tuple-element.25.hidden_ref, bf16[512,2048]{1,0:T(8,128)(2,1)} %weight_ref.3, bf16[4,512,256]{2,1,0:T(8,128)(2,1)} %copy-done), custom_call_target="tpu_custom_call" | custom-call | tf_op jit(solution)/shard_map/keep/pallas_call | solution.py:396
  79.6 2.9 %collective-permute-start.8 = (bf16[4,128,128]{2,1,0:T(8,128)(2,1)S(1)}, bf16[4,128,128]{2,1,0:T(8,128)(2,1)S(1)}, u32[]{:S(2)}, u32[]{:S(2)}) collective-permute-start(bf16[4,128,128]{2,1,0:T(8,128)(2,1)S(1)} %fusion.26), channel_id=1, source_target_pairs={{0,64},{8,72},{16,80},{24,88},{32,96},{40,104},{48,112},{56,120},{... | collective-permute-start | bytes 393224 | tf_op jit(solution)/shard_map/ppermute | solution.py:298
  82.6 6.4 %collective-permute-done.8 = bf16[4,128,128]{2,1,0:T(8,128)(2,1)S(1)} collective-permute-done((bf16[4,128,128]{2,1,0:T(8,128)(2,1)S(1)}, bf16[4,128,128]{2,1,0:T(8,128)(2,1)S(1)}, u32[]{:S(2)}, u32[]{:S(2)}) %collective-permute-start.8) | collective-permute-done | bytes 131104 | tf_op jit(solution)/shard_map/ppermute | solution.py:298
  89.0 4.3 %collective-permute-start.9 = (bf16[4,128,128]{2,1,0:T(8,128)(2,1)S(1)}, bf16[4,128,128]{2,1,0:T(8,128)(2,1)S(1)}, u32[]{:S(2)}, u32[]{:S(2)}) collective-permute-start(bf16[4,128,128]{2,1,0:T(8,128)(2,1)S(1)} %add.93), channel_id=1, source_target_pairs={{0,128},{8,136},{16,144},{24,152},{32,160},{40,168},{48,176},{56,1... | collective-permute-start | bytes 393224 | tf_op jit(solution)/shard_map/ppermute | solution.py:298
  93.3 0.0 copy-done.3
  93.3 0.1 broadcast_compare_fusion
  93.4 3.1 %collective-permute-start.7 = (bf16[512,256]{1,0:T(8,128)(2,1)}, bf16[512,256]{1,0:T(8,128)(2,1)S(1)}, u32[]{:S(2)}, u32[]{:S(2)}) collective-permute-start(bf16[512,256]{1,0:T(8,128)(2,1)} %get-tuple-element.34), channel_id=1, source_target_pairs={{0,4},{1,5},{2,6},{3,7},{4,0},{5,1},{6,2},{7,3},{8,12},{9,13},{10,... | collective-permute-start | bytes 786440 | tf_op jit(solution)/shard_map/ppermute | solution.py:406
  96.4 1.1 %collective-permute-start.6 = (bf16[512,256]{1,0:T(8,128)(2,1)}, bf16[512,256]{1,0:T(8,128)(2,1)S(1)}, u32[]{:S(2)}, u32[]{:S(2)}) collective-permute-start(bf16[512,256]{1,0:T(8,128)(2,1)} %get-tuple-element.33), channel_id=1, source_target_pairs={{0,6},{1,7},{2,0},{3,1},{4,2},{5,3},{6,4},{7,5},{8,14},{9,15},{10,... | collective-permute-start | bytes 786440 | tf_op jit(solution)/shard_map/ppermute | solution.py:406
  97.5 0.9 collective-permute-start.5
  98.4 2.2 %collective-permute-done.9 = bf16[4,128,128]{2,1,0:T(8,128)(2,1)S(1)} collective-permute-done((bf16[4,128,128]{2,1,0:T(8,128)(2,1)S(1)}, bf16[4,128,128]{2,1,0:T(8,128)(2,1)S(1)}, u32[]{:S(2)}, u32[]{:S(2)}) %collective-permute-start.9) | collective-permute-done | bytes 131104 | tf_op jit(solution)/shard_map/ppermute | solution.py:298
  100.6 0.8 select_reduce_fusion
  101.4 4.7 %all-to-all-start.3 = ((bf16[4,128,128]{2,1,0:T(8,128)(2,1)}), bf16[4,128,128]{2,1,0:T(8,128)(2,1)S(1)}, u32[]{:S(2)}, u32[]{:S(2)}) async-start(bf16[4,128,128]{2,1,0:T(8,128)(2,1)} %select_reduce_fusion), calls=%async_computation.3 | async-start | bytes 262144 | tf_op jit(solution)/shard_map/all_to_all | solution.py:304
  106.2 0.0 collective-permute-done.7
  106.2 2.4 %collective-permute-done.6 = bf16[512,256]{1,0:T(8,128)(2,1)S(1)} collective-permute-done((bf16[512,256]{1,0:T(8,128)(2,1)}, bf16[512,256]{1,0:T(8,128)(2,1)S(1)}, u32[]{:S(2)}, u32[]{:S(2)}) %collective-permute-start.6) | collective-permute-done | bytes 262176 | tf_op jit(solution)/shard_map/ppermute | solution.py:406
  108.5 0.0 collective-permute-done.5
  108.5 1.8 %add_convert_fusion = bf16[512,256]{1,0:T(8,128)(2,1)} fusion(bf16[512,256]{1,0:T(8,128)(2,1)S(1)} %collective-permute-done.7, bf16[512,256]{1,0:T(8,128)(2,1)S(1)} %collective-permute-done.6, bf16[512,256]{1,0:T(8,128)(2,1)S(1)} %collective-permute-done.5, bf16[512,256]{1,0:T(8,128)(2,1)} %get-tuple-element.31), kind=kLoop, calls=%fused_computation.9 | loop fusion | flops 1048576 | bytes 1310720 | tf_op jit(solution)/shard_map/convert_element_type | solution.py:418
  110.3 0.4 all-to-all-done.3
  110.7 0.7 bitcast_convert_fusion
  (9 shorter events, 0.2 us)
Async XLA Ops:
  0.6 36.7 %copy-start.4 = (pred[256]{0:T(512)(128)(4,1)S(1)}, pred[256]{0:T(512)(128)(4,1)}, u32[]{:S(2)}) copy-start(pred[256]{0:T(512)(128)(4,1)} %constant.25.clone.1) | copy-start | bytes 772
  26.7 31.4 %copy-start.2 = (f32[4,4,1,128]{3,2,1,0:T(1,128)S(1)}, f32[4,4,1,128]{3,2,1,0:T(1,128)}, u32[]{:S(2)}) copy-start(f32[4,4,1,128]{3,2,1,0:T(1,128)} %get-tuple-element.22) | copy-start | bytes 24580
  26.7 26.6 %all-to-all-start.1 = ((bf16[4,5,128,128]{3,2,1,0:T(8,128)(2,1)}), bf16[4,5,128,128]{3,2,1,0:T(8,128)(2,1)S(1)}, u32[]{:S(2)}, u32[]{:S(2)}) async-start(bf16[4,5,128,128]{3,2,1,0:T(8,128)(2,1)} %get-tuple-element.20), calls=%async_computation.1 | async-start | bytes 1310720 | tf_op jit(solution)/shard_map/all_to_all | solution.py:304
  32.2 5.1 %collective-permute-start = (bf16[128,256]{1,0:T(8,128)(2,1)S(1)}, bf16[128,256]{1,0:T(8,128)(2,1)S(1)}, u32[]{:S(2)}, u32[]{:S(2)}) collective-permute-start(bf16[128,256]{1,0:T(8,128)(2,1)S(1)} %fusion.1), channel_id=1, source_target_pairs={{0,32},{8,40},{16,48},{24,56},{32,64},{40,72},{48,80},{56,88},{64,... | collective-permute-start | bytes 196616 | tf_op jit(solution)/shard_map/ppermute | solution.py:293
  37.5 14.8 %collective-permute-start.1 = (bf16[128,256]{1,0:T(8,128)(2,1)S(1)}, bf16[128,256]{1,0:T(8,128)(2,1)S(1)}, u32[]{:S(2)}, u32[]{:S(2)}) collective-permute-start(bf16[128,256]{1,0:T(8,128)(2,1)S(1)} %fusion.2), channel_id=1, source_target_pairs={{0,32},{8,40},{16,48},{24,56},{32,64},{40,72},{48,80},{56,88},{64,... | collective-permute-start | bytes 196616 | tf_op jit(solution)/shard_map/ppermute | solution.py:293
  41.7 10.5 %collective-permute-start.2 = (bf16[128,128]{1,0:T(8,128)(2,1)S(1)}, bf16[128,128]{1,0:T(8,128)(2,1)S(1)}, u32[]{:S(2)}, u32[]{:S(2)}) collective-permute-start(bf16[128,128]{1,0:T(8,128)(2,1)S(1)} %slice.137), channel_id=1, source_target_pairs={{0,96},{8,104},{16,112},{24,120},{32,128},{40,136},{48,144},{56,15... | collective-permute-start | bytes 98312 | tf_op jit(solution)/shard_map/ppermute | solution.py:293
  53.3 9.3 %all-to-all-start.2 = ((bf16[4,128,128]{2,1,0:T(8,128)(2,1)}), bf16[4,128,128]{2,1,0:T(8,128)(2,1)S(1)}, u32[]{:S(2)}, u32[]{:S(2)}) async-start(bf16[4,128,128]{2,1,0:T(8,128)(2,1)} %pad_maximum_fusion.1), calls=%async_computation.2 | async-start | bytes 262144 | tf_op jit(solution)/shard_map/all_to_all | solution.py:304
  62.6 0.7 copy-start.1
  67.6 7.4 %collective-permute-start.4 = (bf16[4,512,256]{2,1,0:T(8,128)(2,1)}, bf16[4,512,256]{2,1,0:T(8,128)(2,1)S(1)}, u32[]{:S(2)}, u32[]{:S(2)}) collective-permute-start(bf16[4,512,256]{2,1,0:T(8,128)(2,1)} %get-tuple-element.26), channel_id=1, source_target_pairs={{0,1},{1,0},{2,3},{3,2},{4,5},{5,4},{6,7},{7,6},{8,9},{9,8},{10,11... | collective-permute-start | bytes 3145736 | tf_op jit(solution)/shard_map/ppermute | solution.py:395
  68.9 6.0 %collective-permute-start.3 = (bf16[4,128,128]{2,1,0:T(8,128)(2,1)S(1)}, bf16[4,128,128]{2,1,0:T(8,128)(2,1)S(1)}, u32[]{:S(2)}, u32[]{:S(2)}) collective-permute-start(bf16[4,128,128]{2,1,0:T(8,128)(2,1)S(1)} %fusion.4), channel_id=1, source_target_pairs={{0,32},{8,40},{16,48},{24,56},{32,0},{40,8},{48,16},{56,24},{64,96... | collective-permute-start | bytes 393224 | tf_op jit(solution)/shard_map/ppermute | solution.py:298
  75.1 18.2 %copy-start.3 = (s32[4]{0:T(128)S(1)}, s32[4]{0:T(128)}, u32[]{:S(2)}) copy-start(s32[4]{0:T(128)} %param.15) | copy-start | bytes 52
  75.1 1.0 copy-start
  79.6 9.4 %collective-permute-start.8 = (bf16[4,128,128]{2,1,0:T(8,128)(2,1)S(1)}, bf16[4,128,128]{2,1,0:T(8,128)(2,1)S(1)}, u32[]{:S(2)}, u32[]{:S(2)}) collective-permute-start(bf16[4,128,128]{2,1,0:T(8,128)(2,1)S(1)} %fusion.26), channel_id=1, source_target_pairs={{0,64},{8,72},{16,80},{24,88},{32,96},{40,104},{48,112},{56,120},{... | collective-permute-start | bytes 393224 | tf_op jit(solution)/shard_map/ppermute | solution.py:298
  89.0 11.6 %collective-permute-start.9 = (bf16[4,128,128]{2,1,0:T(8,128)(2,1)S(1)}, bf16[4,128,128]{2,1,0:T(8,128)(2,1)S(1)}, u32[]{:S(2)}, u32[]{:S(2)}) collective-permute-start(bf16[4,128,128]{2,1,0:T(8,128)(2,1)S(1)} %add.93), channel_id=1, source_target_pairs={{0,128},{8,136},{16,144},{24,152},{32,160},{40,168},{48,176},{56,1... | collective-permute-start | bytes 393224 | tf_op jit(solution)/shard_map/ppermute | solution.py:298
  93.4 12.8 %collective-permute-start.7 = (bf16[512,256]{1,0:T(8,128)(2,1)}, bf16[512,256]{1,0:T(8,128)(2,1)S(1)}, u32[]{:S(2)}, u32[]{:S(2)}) collective-permute-start(bf16[512,256]{1,0:T(8,128)(2,1)} %get-tuple-element.34), channel_id=1, source_target_pairs={{0,4},{1,5},{2,6},{3,7},{4,0},{5,1},{6,2},{7,3},{8,12},{9,13},{10,... | collective-permute-start | bytes 786440 | tf_op jit(solution)/shard_map/ppermute | solution.py:406
  96.4 12.1 %collective-permute-start.6 = (bf16[512,256]{1,0:T(8,128)(2,1)}, bf16[512,256]{1,0:T(8,128)(2,1)S(1)}, u32[]{:S(2)}, u32[]{:S(2)}) collective-permute-start(bf16[512,256]{1,0:T(8,128)(2,1)} %get-tuple-element.33), channel_id=1, source_target_pairs={{0,6},{1,7},{2,0},{3,1},{4,2},{5,3},{6,4},{7,5},{8,14},{9,15},{10,... | collective-permute-start | bytes 786440 | tf_op jit(solution)/shard_map/ppermute | solution.py:406
  97.5 11.0 %collective-permute-start.5 = (bf16[512,256]{1,0:T(8,128)(2,1)}, bf16[512,256]{1,0:T(8,128)(2,1)S(1)}, u32[]{:S(2)}, u32[]{:S(2)}) collective-permute-start(bf16[512,256]{1,0:T(8,128)(2,1)} %get-tuple-element.32), channel_id=1, source_target_pairs={{0,2},{1,3},{2,4},{3,5},{4,6},{5,7},{6,0},{7,1},{8,10},{9,11},{10,... | collective-permute-start | bytes 786440 | tf_op jit(solution)/shard_map/ppermute | solution.py:406
  101.4 9.3 %all-to-all-start.3 = ((bf16[4,128,128]{2,1,0:T(8,128)(2,1)}), bf16[4,128,128]{2,1,0:T(8,128)(2,1)S(1)}, u32[]{:S(2)}, u32[]{:S(2)}) async-start(bf16[4,128,128]{2,1,0:T(8,128)(2,1)} %select_reduce_fusion), calls=%async_computation.3 | async-start | bytes 262144 | tf_op jit(solution)/shard_map/all_to_all | solution.py:304
where the time goes:
time: 113 us; the launch traced here: 111 us
  starting transfers between devices  43.4 us (38%)
  waiting for transfers between devices  25.1 us (22%)
  Pallas kernels  23.2 us (21%)
  blocking collectives  10.8 us (10%)
  other arithmetic  4.46 us (4%)
  matrix products  1.96 us (2%)
  local copies, waits for them, and re-layouts  1.71 us (2%)
    ppermute x3, starting transfers between devices, shifted(): lax.ppermute(block, 'seq', [(i, i + distance) for i in range(count - dist...  16.4 us
    pallas_call x1, Pallas kernels, program(): pl.pallas_call(kernel, out_shape=(jax.ShapeDtypeStruct((4, local_rows, 2...  15.3 us
    all_to_all x3, starting transfers between devices, traded(): return lax.all_to_all(blocks, 'seq', 0, 0, axis_index_groups=groups)  14.6 us
    ppermute x3, waiting for transfers between devices, swapped(): return lax.ppermute(block, 'seq', [(i, i ^ distance) for i in range(count)])  14.5 us
    all_to_all x1, blocking collectives, traded(): return lax.all_to_all(blocks, 'seq', 0, 0, axis_index_groups=groups)  10.8 us
    ppermute x3, starting transfers between devices, swapped(): return lax.ppermute(block, 'seq', [(i, i ^ distance) for i in range(count)])  7.32 us
    ppermute x3, starting transfers between devices, program(): lax.ppermute(kept[k], 'head', [(i, (i + 2 * k) % COLS) for i in range(COL...  5.08 us
    all_to_all x3, waiting for transfers between devices, traded(): return lax.all_to_all(blocks, 'seq', 0, 0, axis_index_groups=groups)  4.9 us
  transfers between devices with their start and end apart: 13, of which 8 were waited for; matrix products, arithmetic and copies ran while one was open for 5% of the time, Pallas kernels for 0%

commit v1 on v0

--- a/solution.py
+++ b/solution.py
@@ -274,14 +274,13 @@
         send_ref[k] = dot(hidden_ref[...], columns).astype(BF16)
 
 
-def keep_kernel(place_ref, hidden_ref, weight_ref, other_ref, *kept_refs):
-    width = other_ref.shape[2]
+def keep_kernel(place_ref, hidden_ref, weight_ref, kept_ref):
+    width = kept_ref.shape[2]
     place, core = place_ref[0] // 2, place_ref[0] % 2
     for k in range(4):
         j = ((place + k) % 4) * 2 + core
         columns = weight_ref[:, pl.ds(pl.multiple_of(j * width, width), width)]
-        total = dot(hidden_ref[...], columns) + other_ref[k].astype(F32)
-        kept_refs[k][...] = total.astype(BF16)
+        kept_ref[k] = dot(hidden_ref[...], columns).astype(BF16)
 
 
 VMEM = pl.BlockSpec(memory_space=pltpu.VMEM)
@@ -361,11 +360,14 @@
     for y in range(1, 4):
         both = chained(blocks[y], both.astype(BF16))
         prefix.append(both)
-    before = shifted(both.astype(BF16), ROWS)
-    window = chained(prefix.pop().astype(BF16), before).astype(BF16)
-    near = shifted(window, ROWS)
-    far = shifted(window[:, :DV], 3 * ROWS)
-    entering = near[:, :DV].astype(F32) + dot(near[:, DV:], far)
+    total = prefix.pop().astype(BF16)
+    far = shifted(total[:, :DV], 4 * ROWS)
+    third = shifted(total, 3 * ROWS)
+    second = shifted(total, 2 * ROWS)
+    near = shifted(total, ROWS)
+    entering = third[:, :DV].astype(F32) + dot(third[:, DV:], far)
+    entering = second[:, :DV].astype(F32) + dot(second[:, DV:], entering.astype(BF16))
+    entering = near[:, :DV].astype(F32) + dot(near[:, DV:], entering.astype(BF16))
     prefix = jnp.stack(prefix)
     moved = jnp.einsum(
         "yde,ef->ydf", prefix[:, :, DV:].astype(BF16), entering.astype(BF16), preferred_element_type=F32
@@ -379,6 +381,17 @@
     finals = sum(
         closings[y, :4].astype(F32) + flags[y] * moved[y][None] for y in range(ROWS)
     ).astype(BF16)
+
+    other = swapped(finals, 4 * ROWS)
+    finals = finals + other
+    other = swapped(finals, 2 * ROWS)
+    finals = finals + other
+    other = swapped(finals, ROWS)
+    owners = row * ROWS + jnp.arange(ROWS, dtype=jnp.int32)
+    chosen = (decode_owner[None, :] == owners[:, None])[:, :, None, None]
+    finals = finals.astype(F32) + other.astype(F32)
+    parcels = jnp.sum(jnp.where(chosen, finals[None], 0.0), axis=1).astype(BF16)
+    owned = traded(parcels).astype(F32)
 
     width = out_weight.shape[1] // COLS
     there = place[None].astype(jnp.int32)
@@ -391,30 +404,24 @@
         in_specs=[SMEM] + [VMEM] * 4,
         out_specs=(VMEM,) * 2,
         name="send",
+        compiler_params=pltpu.CompilerParams(vmem_limit_bytes=16 << 20),
     )(there, out, arriving, norm_gain[None, :], out_weight)
     incoming = lax.ppermute(outgoing, "head", [(i, i ^ 1) for i in range(COLS)])
     kept = pl.pallas_call(
         keep_kernel,
-        out_shape=(jax.ShapeDtypeStruct((local_rows, width), BF16),) * 4,
-        in_specs=[SMEM] + [VMEM] * 3,
-        out_specs=(VMEM,) * 4,
+        out_shape=jax.ShapeDtypeStruct((4, local_rows, width), BF16),
+        in_specs=[SMEM] + [VMEM] * 2,
+        out_specs=VMEM,
         name="keep",
-    )(there, hidden, out_weight, incoming)
-    finals = finals + swapped(finals, ROWS)
-    finals, *kept = lax.optimization_barrier((finals, *kept))
-    moved = [
-        lax.ppermute(kept[k], "head", [(i, (i + 2 * k) % COLS) for i in range(COLS)])
-        for k in (1, 3, 2)
-    ]
-    for distance in (2 * ROWS, 4 * ROWS):
-        finals = finals + swapped(finals, distance)
-    owners = row * ROWS + jnp.arange(ROWS, dtype=jnp.int32)
-    chosen = (decode_owner[None, :] == owners[:, None])[:, :, None, None]
-    parcels = jnp.sum(jnp.where(chosen, finals[None].astype(F32), 0.0), axis=1).astype(BF16)
-    owned = traded(parcels).astype(F32)
-    mixed = kept[0].astype(F32)
-    for part in moved:
-        mixed = mixed + part.astype(F32)
+        compiler_params=pltpu.CompilerParams(vmem_limit_bytes=16 << 20),
+    )(there, hidden, out_weight)
+    sums = [kept[k].astype(F32) + incoming[k].astype(F32) for k in range(4)]
+    mixed = sums[0]
+    for k in (2, 1, 3):
+        moved = lax.ppermute(
+            sums[k].astype(BF16), "head", [(i, (i + 2 * k) % COLS) for i in range(COLS)]
+        )
+        mixed = mixed + moved.astype(F32)
     return (mixed.astype(BF16), owned[None])
 
 

time: 113 us -> 108 us (0.956)
  blocking collectives: 10.8 us -> 0 us
  starting transfers between devices: 43.4 us -> 50.5 us
  Pallas kernels: 23.2 us -> 18.1 us
  local copies, waits for them, and re-layouts: 1.71 us -> 4.23 us
  other arithmetic: 4.46 us -> 5.81 us
    all_to_all x1 -> x0, blocking collectives: 10.8 us -> none  [traded(): return lax.all_to_all(blocks, 'seq', 0, 0, axis_index_groups=groups)]
    all_to_all x3 -> x4, starting transfers between devices: 14.6 us -> 20.1 us  [traded(): return lax.all_to_all(blocks, 'seq', 0, 0, axis_index_groups=groups)]
    ppermute x3, waiting for transfers between devices: 2.36 us -> 7.08 us  [program(): lax.ppermute(sums[k].astype(BF16), 'head', [(i, (i + 2 * k) % COLS) for i...]
    pallas_call x1, Pallas kernels: 3.51 us -> 0.72 us  [program(): pl.pallas_call(keep_kernel, out_shape=jax.ShapeDtypeStruct((4, local_rows...]
    ppermute x3, waiting for transfers between devices: 14.5 us -> 11.8 us  [swapped(): return lax.ppermute(block, 'seq', [(i, i ^ distance) for i in range(count)])]
    pallas_call x1, Pallas kernels: 4.43 us -> 2.14 us  [program(): pl.pallas_call(send_kernel, out_shape=(jax.ShapeDtypeStruct((local_rows,...]
    ppermute x3 -> x4, waiting for transfers between devices: 3.41 us -> 1.54 us  [shifted(): lax.ppermute(block, 'seq', [(i, i + distance) for i in range(count - dist...]
    unnamed x10 -> x12, local copies, waits for them, and re-layouts: 1.65 us -> 3.45 us
  transfers between devices with their start and end apart: 13 -> 15, of which waited for: 8 -> 7; matrix products, arithmetic and copies ran while one was open for 5% -> 6% of each run, Pallas kernels for 0% -> 1%
where the time goes in v1:
time: 108 us; the launch traced here: 107 us
  starting transfers between devices  50.5 us (47%)
  waiting for transfers between devices  25 us (23%)
  Pallas kernels  18.1 us (17%)
  other arithmetic  5.81 us (5%)
  local copies, waits for them, and re-layouts  4.23 us (4%)
  matrix products  2.11 us (2%)
    all_to_all x4, starting transfers between devices, traded(): return lax.all_to_all(blocks, 'seq', 0, 0, axis_index_groups=groups)  20.1 us
    ppermute x4, starting transfers between devices, shifted(): lax.ppermute(block, 'seq', [(i, i + distance) for i in range(count - dist...  16.2 us
    pallas_call x1, Pallas kernels, program(): pl.pallas_call(kernel, out_shape=(jax.ShapeDtypeStruct((4, local_rows, 2...  15.2 us
    ppermute x3, waiting for transfers between devices, swapped(): return lax.ppermute(block, 'seq', [(i, i ^ distance) for i in range(count)])  11.8 us
    ppermute x3, starting transfers between devices, swapped(): return lax.ppermute(block, 'seq', [(i, i ^ distance) for i in range(count)])  7.79 us
    ppermute x3, waiting for transfers between devices, program(): lax.ppermute(sums[k].astype(BF16), 'head', [(i, (i + 2 * k) % COLS) for i...  7.08 us
    ppermute x3, starting transfers between devices, program(): lax.ppermute(sums[k].astype(BF16), 'head', [(i, (i + 2 * k) % COLS) for i...  6.36 us
    all_to_all x4, waiting for transfers between devices, traded(): return lax.all_to_all(blocks, 'seq', 0, 0, axis_index_groups=groups)  4.5 us
  transfers between devices with their start and end apart: 15, of which 7 were waited for; matrix products, arithmetic and copies ran while one was open for 6% of the time, Pallas kernels for 1%

profile of v1, /device:TPU:8, one launch (start us, length us, event | category | flops | bytes accessed | tf_op | source)
XLA Modules:
  0.0 106.5 jit_solution(4979748493689764733)
XLA Ops:
  0.6 15.2 %local.1 = (f32[4,512,256]{2,1,0:T(8,128)}, bf16[4,2,128,128]{3,2,1,0:T(8,128)(2,1)}, bf16[4,5,128,128]{3,2,1,0:T(8,128)(2,1)}, f32[4,4,1,128]{3,2,1,0:T(1,128)}) custom-call(s32[4]{0:T(128)} %refs_0_.1, s32[1]{0:T(128)} %bitcast.1.refs_1_, bf16[512,256]{1,0:T(8,128)(2,1)} %refs_2_.1, bf16[512,256]{1,0:T(8,128)(2,1)} %refs_3_.1, bf16[512,512]{1,0:T(8,128)(2,1)} %refs_4_.1, ...), custom_call_target="tpu_custom_call" | custom-call | tf_op jit(solution)/shard_map/local/pallas_call | solution.py:336
  15.9 5.6 %all-to-all-start = ((bf16[4,2,128,128]{3,2,1,0:T(8,128)(2,1)}), bf16[4,2,128,128]{3,2,1,0:T(8,128)(2,1)S(1)}, u32[]{:S(2)}, u32[]{:S(2)}) async-start(bf16[4,2,128,128]{3,2,1,0:T(8,128)(2,1)} %get-tuple-element.11), calls=%async_computation | async-start | bytes 524288 | tf_op jit(solution)/shard_map/all_to_all | solution.py:303
  21.5 0.7 fusion.32
  22.2 4.5 %all-to-all-done = bf16[4,2,128,128]{3,2,1,0:T(8,128)(2,1)S(1)} async-done(((bf16[4,2,128,128]{3,2,1,0:T(8,128)(2,1)}), bf16[4,2,128,128]{3,2,1,0:T(8,128)(2,1)S(1)}, u32[]{:S(2)}, u32[]{:S(2)}) %all-to-all-start) | async-done | bytes 262176 | tf_op jit(solution)/shard_map/all_to_all | solution.py:303
  26.7 4.9 %all-to-all-start.1 = ((bf16[4,5,128,128]{3,2,1,0:T(8,128)(2,1)}), bf16[4,5,128,128]{3,2,1,0:T(8,128)(2,1)S(1)}, u32[]{:S(2)}, u32[]{:S(2)}) async-start(bf16[4,5,128,128]{3,2,1,0:T(8,128)(2,1)} %get-tuple-element.12), calls=%async_computation.1 | async-start | bytes 1310720 | tf_op jit(solution)/shard_map/all_to_all | solution.py:303
  31.6 0.1 convolution_add_fusion.3
  31.8 0.1 convolution_add_fusion.2
  31.9 0.1 fusion.1
  32.1 5.9 %collective-permute-start.2 = (bf16[128,256]{1,0:T(8,128)(2,1)S(1)}, bf16[128,256]{1,0:T(8,128)(2,1)S(1)}, u32[]{:S(2)}, u32[]{:S(2)}) collective-permute-start(bf16[128,256]{1,0:T(8,128)(2,1)S(1)} %fusion.1), channel_id=1, source_target_pairs={{0,96},{8,104},{16,112},{24,120},{32,128},{40,136},{48,144},{56,15... | collective-permute-start | bytes 196616 | tf_op jit(solution)/shard_map/ppermute | solution.py:292
  38.0 0.0 copy-start
  38.0 0.0 copy-start.4
  38.0 5.2 %collective-permute-start = (bf16[128,256]{1,0:T(8,128)(2,1)S(1)}, bf16[128,256]{1,0:T(8,128)(2,1)S(1)}, u32[]{:S(2)}, u32[]{:S(2)}) collective-permute-start(bf16[128,256]{1,0:T(8,128)(2,1)S(1)} %fusion.1), channel_id=1, source_target_pairs={{0,32},{8,40},{16,48},{24,56},{32,64},{40,72},{48,80},{56,88},{64,... | collective-permute-start | bytes 196616 | tf_op jit(solution)/shard_map/ppermute | solution.py:292
  43.2 3.4 %collective-permute-start.1 = (bf16[128,256]{1,0:T(8,128)(2,1)S(1)}, bf16[128,256]{1,0:T(8,128)(2,1)S(1)}, u32[]{:S(2)}, u32[]{:S(2)}) collective-permute-start(bf16[128,256]{1,0:T(8,128)(2,1)S(1)} %fusion.1), channel_id=1, source_target_pairs={{0,64},{8,72},{16,80},{24,88},{32,96},{40,104},{48,112},{56,120},{... | collective-permute-start | bytes 196616 | tf_op jit(solution)/shard_map/ppermute | solution.py:292
  46.6 1.8 %collective-permute-start.3 = (bf16[128,128]{1,0:T(8,128)(2,1)S(1)}, bf16[128,128]{1,0:T(8,128)(2,1)S(1)}, u32[]{:S(2)}, u32[]{:S(2)}) collective-permute-start(bf16[128,128]{1,0:T(8,128)(2,1)S(1)} %slice.182), channel_id=1, source_target_pairs={{0,128},{8,136},{16,144},{24,152},{32,160},{40,168},{48,176},{56,1... | collective-permute-start | bytes 98312 | tf_op jit(solution)/shard_map/ppermute | solution.py:292
  48.4 1.5 %collective-permute-done.3 = bf16[128,128]{1,0:T(8,128)(2,1)S(1)} collective-permute-done((bf16[128,128]{1,0:T(8,128)(2,1)S(1)}, bf16[128,128]{1,0:T(8,128)(2,1)S(1)}, u32[]{:S(2)}, u32[]{:S(2)}) %collective-permute-start.3) | collective-permute-done | bytes 32800 | tf_op jit(solution)/shard_map/ppermute | solution.py:292
  50.0 0.0 collective-permute-done.2
  50.0 0.1 fusion.22
  50.1 0.0 collective-permute-done
  50.1 0.0 collective-permute-done.1
  50.1 0.3 add_convert_fusion.3
  50.4 0.2 fusion
  50.6 0.7 pad_maximum_fusion.1
  51.2 0.0 all-to-all-done.1
  51.2 4.8 %all-to-all-start.2 = ((bf16[4,128,128]{2,1,0:T(8,128)(2,1)}), bf16[4,128,128]{2,1,0:T(8,128)(2,1)S(1)}, u32[]{:S(2)}, u32[]{:S(2)}) async-start(bf16[4,128,128]{2,1,0:T(8,128)(2,1)} %pad_maximum_fusion.1), calls=%async_computation.2 | async-start | bytes 262144 | tf_op jit(solution)/shard_map/all_to_all | solution.py:303
  56.0 1.1 %fusion.12 = f32[4,128,128]{2,1,0:T(8,128)S(1)} fusion(bf16[4,128,128]{2,1,0:T(8,128)(2,1)} %pad_maximum_fusion.1, bf16[4,5,128,128]{3,2,1,0:T(8,128)(2,1)S(1)} %all-to-all-done.1), kind=kOutput, calls=%fused_computation.30 | convolution fusion | flops 16777216 | bytes 524288 | tf_op jit(solution)/shard_map/yde,yef->ydf/dot_general | solution.py:380
  57.2 0.2 fusion.9
  57.3 6.3 %collective-permute-start.8 = (bf16[4,128,128]{2,1,0:T(8,128)(2,1)S(1)}, bf16[4,128,128]{2,1,0:T(8,128)(2,1)S(1)}, u32[]{:S(2)}, u32[]{:S(2)}) collective-permute-start(bf16[4,128,128]{2,1,0:T(8,128)(2,1)S(1)} %fusion.9), channel_id=1, source_target_pairs={{0,128},{8,136},{16,144},{24,152},{32,160},{40,168},{48,176},{56,1... | collective-permute-start | bytes 393224 | tf_op jit(solution)/shard_map/ppermute | solution.py:297
  63.7 0.0 all-to-all-done.2.arriving_ref
  63.7 0.0 copy-done
  63.7 0.0 copy-done.4
  63.7 0.0 copy-start.1
  63.7 1.6 %copy-done.1 = f32[4,512,256]{2,1,0:T(8,128)S(1)} copy-done((f32[4,512,256]{2,1,0:T(8,128)S(1)}, f32[4,512,256]{2,1,0:T(8,128)}, u32[]{:S(2)}) %copy-start.1) | copy-done | bytes 2097176
  65.3 0.0 copy-start.5
  65.3 2.1 %send.1 = (bf16[512,512]{1,0:T(8,128)(2,1)S(1)}, bf16[4,512,256]{2,1,0:T(8,128)(2,1)}) custom-call(s32[1]{0:T(128)} %bitcast.place_ref, f32[4,512,256]{2,1,0:T(8,128)S(1)} %copy-done.1, bf16[4,128,128]{2,1,0:T(8,128)(2,1)S(1)} %all-to-all-done.2.arriving_ref, f32[1,128]{1,0:T(1,128)S(1)} %bitcast.86, bf16[512,2048]{1,0:T(8,128)(2,1)S(1)} %copy-done), custom_call_target="tpu_custom_call" | custom-call | tf_op jit(solution)/shard_map/send/pallas_call | solution.py:398
  67.4 0.0 copy-start.2
  67.4 0.8 copy-done.2
  68.2 0.0 collective-permute-start.4
  68.2 0.0 collective-permute-done.8
  68.2 0.2 fusion.35
  68.4 1.4 %collective-permute-start.9 = (bf16[4,128,128]{2,1,0:T(8,128)(2,1)S(1)}, bf16[4,128,128]{2,1,0:T(8,128)(2,1)S(1)}, u32[]{:S(2)}, u32[]{:S(2)}) collective-permute-start(bf16[4,128,128]{2,1,0:T(8,128)(2,1)S(1)} %fusion.35), channel_id=1, source_target_pairs={{0,64},{8,72},{16,80},{24,88},{32,96},{40,104},{48,112},{56,120},{... | collective-permute-start | bytes 393224 | tf_op jit(solution)/shard_map/ppermute | solution.py:297
  69.8 8.2 %collective-permute-done.9 = bf16[4,128,128]{2,1,0:T(8,128)(2,1)S(1)} collective-permute-done((bf16[4,128,128]{2,1,0:T(8,128)(2,1)S(1)}, bf16[4,128,128]{2,1,0:T(8,128)(2,1)S(1)}, u32[]{:S(2)}, u32[]{:S(2)}) %collective-permute-start.9) | collective-permute-done | bytes 131104 | tf_op jit(solution)/shard_map/ppermute | solution.py:297
  78.0 0.1 collective-permute-start.10
  78.2 0.0 copy-done.5
  78.2 0.1 broadcast_compare_fusion
  78.2 0.0 copy-start.3
  78.2 1.0 copy-done.3
  79.3 0.7 keep.1
  80.0 3.6 %collective-permute-done.10 = bf16[4,128,128]{2,1,0:T(8,128)(2,1)S(1)} collective-permute-done((bf16[4,128,128]{2,1,0:T(8,128)(2,1)S(1)}, bf16[4,128,128]{2,1,0:T(8,128)(2,1)S(1)}, u32[]{:S(2)}, u32[]{:S(2)}) %collective-permute-start.10) | collective-permute-done | bytes 131104 | tf_op jit(solution)/shard_map/ppermute | solution.py:297
  83.6 0.8 select_reduce_fusion
  84.5 4.8 %all-to-all-start.3 = ((bf16[4,128,128]{2,1,0:T(8,128)(2,1)}), bf16[4,128,128]{2,1,0:T(8,128)(2,1)S(1)}, u32[]{:S(2)}, u32[]{:S(2)}) async-start(bf16[4,128,128]{2,1,0:T(8,128)(2,1)} %select_reduce_fusion), calls=%async_computation.3 | async-start | bytes 262144 | tf_op jit(solution)/shard_map/all_to_all | solution.py:303
  89.3 0.0 collective-permute-done.4
  89.3 1.3 %fusion.5 = (bf16[512,256]{1,0:T(8,128)(2,1)S(1)}, bf16[512,256]{1,0:T(8,128)(2,1)S(1)}, bf16[512,256]{1,0:T(8,128)(2,1)S(1)}) fusion(bf16[4,512,256]{2,1,0:T(8,128)(2,1)} %collective-permute-done.4, bf16[4,512,256]{2,1,0:T(8,128)(2,1)S(1)} %keep.1), kind=kLoop, calls=%fused_computation.15 | loop fusion | flops 1572864 | bytes 2359296 | tf_op jit(solution)/shard_map/convert_element_type | solution.py:422
  90.5 3.1 %collective-permute-start.5 = (bf16[512,256]{1,0:T(8,128)(2,1)S(1)}, bf16[512,256]{1,0:T(8,128)(2,1)S(1)}, u32[]{:S(2)}, u32[]{:S(2)}) collective-permute-start(bf16[512,256]{1,0:T(8,128)(2,1)S(1)} %get-tuple-element.18), channel_id=1, source_target_pairs={{0,4},{1,5},{2,6},{3,7},{4,0},{5,1},{6,2},{7,3},{8,12},{9,13},{10,... | collective-permute-start | bytes 786440 | tf_op jit(solution)/shard_map/ppermute | solution.py:421
  93.7 0.6 collective-permute-start.6
  94.3 2.7 %collective-permute-start.7 = (bf16[512,256]{1,0:T(8,128)(2,1)S(1)}, bf16[512,256]{1,0:T(8,128)(2,1)S(1)}, u32[]{:S(2)}, u32[]{:S(2)}) collective-permute-start(bf16[512,256]{1,0:T(8,128)(2,1)S(1)} %get-tuple-element.19), channel_id=1, source_target_pairs={{0,6},{1,7},{2,0},{3,1},{4,2},{5,3},{6,4},{7,5},{8,14},{9,15},{10,... | collective-permute-start | bytes 786440 | tf_op jit(solution)/shard_map/ppermute | solution.py:421
  96.9 0.0 all-to-all-done.3
  96.9 0.7 bitcast_convert_fusion
  97.6 3.7 %collective-permute-done.5 = bf16[512,256]{1,0:T(8,128)(2,1)S(1)} collective-permute-done((bf16[512,256]{1,0:T(8,128)(2,1)S(1)}, bf16[512,256]{1,0:T(8,128)(2,1)S(1)}, u32[]{:S(2)}, u32[]{:S(2)}) %collective-permute-start.5) | collective-permute-done | bytes 262176 | tf_op jit(solution)/shard_map/ppermute | solution.py:421
  101.3 3.3 %collective-permute-done.6 = bf16[512,256]{1,0:T(8,128)(2,1)S(1)} collective-permute-done((bf16[512,256]{1,0:T(8,128)(2,1)S(1)}, bf16[512,256]{1,0:T(8,128)(2,1)S(1)}, u32[]{:S(2)}, u32[]{:S(2)}) %collective-permute-start.6) | collective-permute-done | bytes 262176 | tf_op jit(solution)/shard_map/ppermute | solution.py:421
  104.6 0.1 collective-permute-done.7
  104.7 1.8 %fusion.4 = bf16[512,256]{1,0:T(8,128)(2,1)} fusion(bf16[512,256]{1,0:T(8,128)(2,1)S(1)} %collective-permute-done.7, bf16[512,256]{1,0:T(8,128)(2,1)S(1)} %collective-permute-done.6, bf16[512,256]{1,0:T(8,128)(2,1)S(1)} %collective-permute-done.5, bf16[4,512,256]{2,1,0:T(8,128)(2,1)} %collective-permute-done.4, bf16[4,512,256]{2,1,0:T(8,128)(2,1)S(1)} %keep.1), kind=kLoop, calls=%fused_computation.10 | loop fusion | flops 1310720 | bytes 1572864 | tf_op jit(solution)/shard_map/convert_element_type | solution.py:425
  (8 shorter events, 0.2 us)
Async XLA Ops:
  15.9 10.8 %all-to-all-start = ((bf16[4,2,128,128]{3,2,1,0:T(8,128)(2,1)}), bf16[4,2,128,128]{3,2,1,0:T(8,128)(2,1)S(1)}, u32[]{:S(2)}, u32[]{:S(2)}) async-start(bf16[4,2,128,128]{3,2,1,0:T(8,128)(2,1)} %get-tuple-element.11), calls=%async_computation | async-start | bytes 524288 | tf_op jit(solution)/shard_map/all_to_all | solution.py:303
  26.7 24.6 %all-to-all-start.1 = ((bf16[4,5,128,128]{3,2,1,0:T(8,128)(2,1)}), bf16[4,5,128,128]{3,2,1,0:T(8,128)(2,1)S(1)}, u32[]{:S(2)}, u32[]{:S(2)}) async-start(bf16[4,5,128,128]{3,2,1,0:T(8,128)(2,1)} %get-tuple-element.12), calls=%async_computation.1 | async-start | bytes 1310720 | tf_op jit(solution)/shard_map/all_to_all | solution.py:303
  32.1 17.9 %collective-permute-start.2 = (bf16[128,256]{1,0:T(8,128)(2,1)S(1)}, bf16[128,256]{1,0:T(8,128)(2,1)S(1)}, u32[]{:S(2)}, u32[]{:S(2)}) collective-permute-start(bf16[128,256]{1,0:T(8,128)(2,1)S(1)} %fusion.1), channel_id=1, source_target_pairs={{0,96},{8,104},{16,112},{24,120},{32,128},{40,136},{48,144},{56,15... | collective-permute-start | bytes 196616 | tf_op jit(solution)/shard_map/ppermute | solution.py:292
  38.0 25.7 %copy-start = (bf16[512,2048]{1,0:T(8,128)(2,1)S(1)}, bf16[512,2048]{1,0:T(8,128)(2,1)}, u32[]{:S(2)}) copy-start(bf16[512,2048]{1,0:T(8,128)(2,1)} %weight_ref.3) | copy-start | bytes 6291460
  38.0 25.7 %copy-start.4 = (f32[128]{0:T(128)S(1)}, f32[128]{0:T(128)}, u32[]{:S(2)}) copy-start(f32[128]{0:T(128)} %param.16) | copy-start | bytes 1540
  38.0 12.1 %collective-permute-start = (bf16[128,256]{1,0:T(8,128)(2,1)S(1)}, bf16[128,256]{1,0:T(8,128)(2,1)S(1)}, u32[]{:S(2)}, u32[]{:S(2)}) collective-permute-start(bf16[128,256]{1,0:T(8,128)(2,1)S(1)} %fusion.1), channel_id=1, source_target_pairs={{0,32},{8,40},{16,48},{24,56},{32,64},{40,72},{48,80},{56,88},{64,... | collective-permute-start | bytes 196616 | tf_op jit(solution)/shard_map/ppermute | solution.py:292
  43.2 6.9 %collective-permute-start.1 = (bf16[128,256]{1,0:T(8,128)(2,1)S(1)}, bf16[128,256]{1,0:T(8,128)(2,1)S(1)}, u32[]{:S(2)}, u32[]{:S(2)}) collective-permute-start(bf16[128,256]{1,0:T(8,128)(2,1)S(1)} %fusion.1), channel_id=1, source_target_pairs={{0,64},{8,72},{16,80},{24,88},{32,96},{40,104},{48,112},{56,120},{... | collective-permute-start | bytes 196616 | tf_op jit(solution)/shard_map/ppermute | solution.py:292
  46.6 3.4 %collective-permute-start.3 = (bf16[128,128]{1,0:T(8,128)(2,1)S(1)}, bf16[128,128]{1,0:T(8,128)(2,1)S(1)}, u32[]{:S(2)}, u32[]{:S(2)}) collective-permute-start(bf16[128,128]{1,0:T(8,128)(2,1)S(1)} %slice.182), channel_id=1, source_target_pairs={{0,128},{8,136},{16,144},{24,152},{32,160},{40,168},{48,176},{56,1... | collective-permute-start | bytes 98312 | tf_op jit(solution)/shard_map/ppermute | solution.py:292
  51.2 12.4 %all-to-all-start.2 = ((bf16[4,128,128]{2,1,0:T(8,128)(2,1)}), bf16[4,128,128]{2,1,0:T(8,128)(2,1)S(1)}, u32[]{:S(2)}, u32[]{:S(2)}) async-start(bf16[4,128,128]{2,1,0:T(8,128)(2,1)} %pad_maximum_fusion.1), calls=%async_computation.2 | async-start | bytes 262144 | tf_op jit(solution)/shard_map/all_to_all | solution.py:303
  57.3 10.9 %collective-permute-start.8 = (bf16[4,128,128]{2,1,0:T(8,128)(2,1)S(1)}, bf16[4,128,128]{2,1,0:T(8,128)(2,1)S(1)}, u32[]{:S(2)}, u32[]{:S(2)}) collective-permute-start(bf16[4,128,128]{2,1,0:T(8,128)(2,1)S(1)} %fusion.9), channel_id=1, source_target_pairs={{0,128},{8,136},{16,144},{24,152},{32,160},{40,168},{48,176},{56,1... | collective-permute-start | bytes 393224 | tf_op jit(solution)/shard_map/ppermute | solution.py:297
  63.7 1.6 %copy-start.1 = (f32[4,512,256]{2,1,0:T(8,128)S(1)}, f32[4,512,256]{2,1,0:T(8,128)}, u32[]{:S(2)}) copy-start(f32[4,512,256]{2,1,0:T(8,128)} %get-tuple-element.10.out_ref) | copy-start | bytes 6291460
  65.3 12.9 %copy-start.5 = (s32[4]{0:T(128)S(1)}, s32[4]{0:T(128)}, u32[]{:S(2)}) copy-start(s32[4]{0:T(128)} %param.15) | copy-start | bytes 52
  67.4 0.8 copy-start.2
  68.2 21.1 %collective-permute-start.4 = (bf16[4,512,256]{2,1,0:T(8,128)(2,1)}, bf16[4,512,256]{2,1,0:T(8,128)(2,1)}, u32[]{:S(2)}, u32[]{:S(2)}) collective-permute-start(bf16[4,512,256]{2,1,0:T(8,128)(2,1)} %get-tuple-element.15), channel_id=1, source_target_pairs={{0,1},{1,0},{2,3},{3,2},{4,5},{5,4},{6,7},{7,6},{8,9},{9,8},{10,11... | collective-permute-start | bytes 3145736 | tf_op jit(solution)/shard_map/ppermute | solution.py:409
  68.4 9.6 %collective-permute-start.9 = (bf16[4,128,128]{2,1,0:T(8,128)(2,1)S(1)}, bf16[4,128,128]{2,1,0:T(8,128)(2,1)S(1)}, u32[]{:S(2)}, u32[]{:S(2)}) collective-permute-start(bf16[4,128,128]{2,1,0:T(8,128)(2,1)S(1)} %fusion.35), channel_id=1, source_target_pairs={{0,64},{8,72},{16,80},{24,88},{32,96},{40,104},{48,112},{56,120},{... | collective-permute-start | bytes 393224 | tf_op jit(solution)/shard_map/ppermute | solution.py:297
  78.0 5.6 %collective-permute-start.10 = (bf16[4,128,128]{2,1,0:T(8,128)(2,1)S(1)}, bf16[4,128,128]{2,1,0:T(8,128)(2,1)S(1)}, u32[]{:S(2)}, u32[]{:S(2)}) collective-permute-start(bf16[4,128,128]{2,1,0:T(8,128)(2,1)S(1)} %add.120), channel_id=1, source_target_pairs={{0,32},{8,40},{16,48},{24,56},{32,0},{40,8},{48,16},{56,24},{64,96... | collective-permute-start | bytes 393224 | tf_op jit(solution)/shard_map/ppermute | solution.py:297
  78.2 1.0 copy-start.3
  84.5 12.5 %all-to-all-start.3 = ((bf16[4,128,128]{2,1,0:T(8,128)(2,1)}), bf16[4,128,128]{2,1,0:T(8,128)(2,1)S(1)}, u32[]{:S(2)}, u32[]{:S(2)}) async-start(bf16[4,128,128]{2,1,0:T(8,128)(2,1)} %select_reduce_fusion), calls=%async_computation.3 | async-start | bytes 262144 | tf_op jit(solution)/shard_map/all_to_all | solution.py:303
  90.5 10.8 %collective-permute-start.5 = (bf16[512,256]{1,0:T(8,128)(2,1)S(1)}, bf16[512,256]{1,0:T(8,128)(2,1)S(1)}, u32[]{:S(2)}, u32[]{:S(2)}) collective-permute-start(bf16[512,256]{1,0:T(8,128)(2,1)S(1)} %get-tuple-element.18), channel_id=1, source_target_pairs={{0,4},{1,5},{2,6},{3,7},{4,0},{5,1},{6,2},{7,3},{8,12},{9,13},{10,... | collective-permute-start | bytes 786440 | tf_op jit(solution)/shard_map/ppermute | solution.py:421
  93.7 11.0 %collective-permute-start.6 = (bf16[512,256]{1,0:T(8,128)(2,1)S(1)}, bf16[512,256]{1,0:T(8,128)(2,1)S(1)}, u32[]{:S(2)}, u32[]{:S(2)}) collective-permute-start(bf16[512,256]{1,0:T(8,128)(2,1)S(1)} %get-tuple-element.20), channel_id=1, source_target_pairs={{0,2},{1,3},{2,4},{3,5},{4,6},{5,7},{6,0},{7,1},{8,10},{9,11},{10,... | collective-permute-start | bytes 786440 | tf_op jit(solution)/shard_map/ppermute | solution.py:421
  94.3 10.5 %collective-permute-start.7 = (bf16[512,256]{1,0:T(8,128)(2,1)S(1)}, bf16[512,256]{1,0:T(8,128)(2,1)S(1)}, u32[]{:S(2)}, u32[]{:S(2)}) collective-permute-start(bf16[512,256]{1,0:T(8,128)(2,1)S(1)} %get-tuple-element.19), channel_id=1, source_target_pairs={{0,6},{1,7},{2,0},{3,1},{4,2},{5,3},{6,4},{7,5},{8,14},{9,15},{10,... | collective-permute-start | bytes 786440 | tf_op jit(solution)/shard_map/ppermute | solution.py:421

commit v2 on v1

--- a/solution.py
+++ b/solution.py
@@ -60,6 +60,7 @@
     gate_ref,
     rate_ref,
     out_ref,
+    link_ref,
     block_ref,
     close_ref,
     flag_ref,
@@ -182,9 +183,10 @@
     for p in range(4):
         total = total + lengths_ref[p]
         finish.append(total)
-    row_first = (position_ref[0] // ROWS) * ROWS
+    inner = position_ref[0] % ROWS
+    row_first = position_ref[0] - inner
     for y in range(ROWS):
-        start = (row_first + y) * number
+        start = (row_first + (inner + y) % ROWS) * number
         for p in range(4):
             active = finish[p] > start
             if p > 0:
@@ -240,16 +242,18 @@
                 dot(score_s[unit], high) + dot(score_s[unit], low)
             )
             for r in range(2):
-                out_ref[2 * c + r, rows, :] = output[tops[r]]
+                out_ref[2 * c + r, rows, :] = output[tops[r], :DV]
+                link_ref[2 * c + r, rows, :] = output[tops[r], DV:].astype(BF16)
 
         for p in range(4):
 
             @pl.when(ident + 1 == finish[p])
             def _(p=p):
                 for h in range(4):
-                    close_ref[h, p] = state_s[h, :, :DV].astype(BF16)
-                    close_ref[h, 4] = (
-                        close_ref[h, 4].astype(F32) + state_s[h, :, DV:]
+                    slot = (inner + ROWS - h) % ROWS
+                    close_ref[slot, p] = state_s[h, :, :DV].astype(BF16)
+                    close_ref[slot, 4] = (
+                        close_ref[slot, 4].astype(F32) + state_s[h, :, DV:]
                     ).astype(BF16)
 
         return carry
@@ -260,10 +264,12 @@
         block_ref[h, 1] = state_s[h, :, DV:].astype(BF16)
 
 
-def send_kernel(place_ref, out_ref, arriving_ref, gain_ref, weight_ref, hidden_ref, send_ref):
+def send_kernel(
+    place_ref, out_ref, link_ref, arriving_ref, gain_ref, weight_ref, hidden_ref, send_ref
+):
     gain = gain_ref[...]
     for h in range(4):
-        output = out_ref[h, :, :DV] + dot_left(halves(out_ref[h, :, DV:]), arriving_ref[h])
+        output = out_ref[h] + dot(link_ref[h], arriving_ref[h])
         scale = lax.rsqrt(jnp.mean(output * output, axis=1, keepdims=True) + 1e-06)
         hidden_ref[:, h * DV : (h + 1) * DV] = (output * scale * gain).astype(BF16)
     width = send_ref.shape[2]
@@ -333,16 +339,17 @@
         local_kernel(number, *refs)
 
     units = 2 * number
-    out, block, closing, flags = pl.pallas_call(
+    out, links, block, closing, flags = pl.pallas_call(
         kernel,
         out_shape=(
-            jax.ShapeDtypeStruct((4, local_rows, 2 * DV), F32),
+            jax.ShapeDtypeStruct((4, local_rows, DV), F32),
+            jax.ShapeDtypeStruct((4, local_rows, DK), BF16),
             jax.ShapeDtypeStruct((4, 2, DK, DV), BF16),
             jax.ShapeDtypeStruct((4, 5, DK, DV), BF16),
             jax.ShapeDtypeStruct((ROWS, 4, 1, DV), F32),
         ),
         in_specs=[SMEM] * 2 + [VMEM] * 5,
-        out_specs=(VMEM,) * 4,
+        out_specs=(VMEM,) * 5,
         scratch_shapes=[
             pltpu.VMEM((units, 2, PAIR, DK), BF16),
             pltpu.VMEM((units, PAIR, DK), F32),
@@ -354,14 +361,19 @@
     )(prompt_stretches, here, queries, key_vectors, values, gate_log, write_rate)
 
     blocks = traded(block)
-    closings = traded(closing)
+    count = lax.axis_size("seq")
+    closings = [closing[0]]
+    for k in range(1, ROWS):
+        route = [(i, (i // ROWS) * ROWS + (i - k) % ROWS) for i in range(count)]
+        closings.append(lax.ppermute(closing[k], "seq", route))
     both = jnp.concatenate([blocks[0, 0], blocks[0, 1]], axis=1).astype(F32)
     prefix = [both]
     for y in range(1, 4):
         both = chained(blocks[y], both.astype(BF16))
         prefix.append(both)
     total = prefix.pop().astype(BF16)
-    far = shifted(total[:, :DV], 4 * ROWS)
+    last = dot(blocks[3, 1], prefix[-1][:, :DV].astype(BF16)) + blocks[3, 0].astype(F32)
+    far = shifted(last.astype(BF16), 4 * ROWS)
     third = shifted(total, 3 * ROWS)
     second = shifted(total, 2 * ROWS)
     near = shifted(total, ROWS)
@@ -373,27 +385,22 @@
         "yde,ef->ydf", prefix[:, :, DV:].astype(BF16), entering.astype(BF16), preferred_element_type=F32
     )
     starts = jnp.concatenate([entering[None], prefix[:, :, :DV] + moved]).astype(BF16)
-    starts, closings = lax.optimization_barrier((starts, closings))
     arriving = traded(starts)
 
     row = position // ROWS
-    moved = jnp.einsum("yde,yef->ydf", closings[:, 4], starts, preferred_element_type=F32)
+    turned = lax.dynamic_slice_in_dim(
+        jnp.concatenate([starts, starts]), position % ROWS, ROWS, axis=0
+    )
     finals = sum(
-        closings[y, :4].astype(F32) + flags[y] * moved[y][None] for y in range(ROWS)
+        closings[k][:4].astype(F32) + flags[k] * dot(closings[k][4], turned[k])[None]
+        for k in range(ROWS)
     ).astype(BF16)
 
     other = swapped(finals, 4 * ROWS)
     finals = finals + other
     other = swapped(finals, 2 * ROWS)
-    finals = finals + other
-    other = swapped(finals, ROWS)
-    owners = row * ROWS + jnp.arange(ROWS, dtype=jnp.int32)
-    chosen = (decode_owner[None, :] == owners[:, None])[:, :, None, None]
-    finals = finals.astype(F32) + other.astype(F32)
-    parcels = jnp.sum(jnp.where(chosen, finals[None], 0.0), axis=1).astype(BF16)
-    owned = traded(parcels).astype(F32)
-
     width = out_weight.shape[1] // COLS
+    out_weight = pltpu.with_memory_space_constraint(out_weight, pltpu.HBM)
     there = place[None].astype(jnp.int32)
     hidden, outgoing = pl.pallas_call(
         send_kernel,
@@ -401,11 +408,11 @@
             jax.ShapeDtypeStruct((local_rows, 4 * DV), BF16),
             jax.ShapeDtypeStruct((4, local_rows, width), BF16),
         ),
-        in_specs=[SMEM] + [VMEM] * 4,
+        in_specs=[SMEM] + [VMEM] * 5,
         out_specs=(VMEM,) * 2,
         name="send",
         compiler_params=pltpu.CompilerParams(vmem_limit_bytes=16 << 20),
-    )(there, out, arriving, norm_gain[None, :], out_weight)
+    )(there, out, links, arriving, norm_gain[None, :], out_weight)
     incoming = lax.ppermute(outgoing, "head", [(i, i ^ 1) for i in range(COLS)])
     kept = pl.pallas_call(
         keep_kernel,
@@ -416,10 +423,20 @@
         compiler_params=pltpu.CompilerParams(vmem_limit_bytes=16 << 20),
     )(there, hidden, out_weight)
     sums = [kept[k].astype(F32) + incoming[k].astype(F32) for k in range(4)]
+    parts = [sums[k].astype(BF16) for k in range(4)]
+    finals, _ = lax.optimization_barrier((finals, parts[2]))
+    finals = finals + other
+    other = swapped(finals, ROWS)
+    owners = row * ROWS + jnp.arange(ROWS, dtype=jnp.int32)
+    chosen = (decode_owner[None, :] == owners[:, None])[:, :, None, None]
+    finals = finals.astype(F32) + other.astype(F32)
+    parcels = jnp.sum(jnp.where(chosen, finals[None], 0.0), axis=1).astype(BF16)
+    owned = traded(parcels).astype(F32)
+
     mixed = sums[0]
     for k in (2, 1, 3):
         moved = lax.ppermute(
-            sums[k].astype(BF16), "head", [(i, (i + 2 * k) % COLS) for i in range(COLS)]
+            parts[k], "head", [(i, (i + 2 * k) % COLS) for i in range(COLS)]
         )
         mixed = mixed + moved.astype(F32)
     return (mixed.astype(BF16), owned[None])

time: 108 us -> 119 us (1.10)
  starting transfers between devices: 50.5 us -> 54.3 us
  waiting for transfers between devices: 25 us -> 28.1 us
  matrix products: 2.11 us -> 4.71 us
  Pallas kernels: 18.1 us -> 20 us
  local copies, waits for them, and re-layouts: 4.23 us -> 2.57 us
    all_to_all x4 -> x3, starting transfers between devices: 20.1 us -> 15.1 us  [traded(): return lax.all_to_all(blocks, 'seq', 0, 0, axis_index_groups=groups)]
    ppermute x3 -> x6, starting transfers between devices: 6.36 us -> 11.1 us  [the longest x3 6.28 us: program(): lax.ppermute(parts[k], 'head', [(i, (i + 2 * k) % COLS) for i in range(CO...]
    ppermute x3, starting transfers between devices: 7.79 us -> 12 us  [swapped(): return lax.ppermute(block, 'seq', [(i, i ^ distance) for i in range(count)])]
    ppermute x3, waiting for transfers between devices: 11.8 us -> 15.8 us  [swapped(): return lax.ppermute(block, 'seq', [(i, i ^ distance) for i in range(count)])]
    dot_general x5 -> x10, matrix products: 0.84 us -> 4.54 us  [dot(): return lax.dot_general(a, b, dims, preferred_element_type=F32)]
    unnamed x12 -> x8, local copies, waits for them, and re-layouts: 3.45 us -> 0.02 us
    squeeze x0 -> x1, local copies, waits for them, and re-layouts: none -> 1.86 us  [program(): closings.append(lax.ppermute(closing[k], 'seq', route))]
    ppermute x4, waiting for transfers between devices: 1.54 us -> 3.3 us  [shifted(): lax.ppermute(block, 'seq', [(i, i + distance) for i in range(count - dist...]
  transfers between devices with their start and end apart: 15 -> 17, of which waited for: 7 -> 9; matrix products, arithmetic and copies ran while one was open for 6% -> 10% of each run, Pallas kernels for 1% -> 2%
where the time goes in v2:
time: 119 us; the launch traced here: 117 us
  starting transfers between devices  54.3 us (46%)
  waiting for transfers between devices  28.1 us (24%)
  Pallas kernels  20 us (17%)
  other arithmetic  6.89 us (6%)
  matrix products  4.71 us (4%)
  local copies, waits for them, and re-layouts  2.57 us (2%)
    ppermute x4, starting transfers between devices, shifted(): lax.ppermute(block, 'seq', [(i, i + distance) for i in range(count - dist...  16 us
    ppermute x3, waiting for transfers between devices, swapped(): return lax.ppermute(block, 'seq', [(i, i ^ distance) for i in range(count)])  15.8 us
    all_to_all x3, starting transfers between devices, traded(): return lax.all_to_all(blocks, 'seq', 0, 0, axis_index_groups=groups)  15.1 us
    pallas_call x1, Pallas kernels, program(): pl.pallas_call(kernel, out_shape=(jax.ShapeDtypeStruct((4, local_rows, DV...  15.1 us
    ppermute x3, starting transfers between devices, swapped(): return lax.ppermute(block, 'seq', [(i, i ^ distance) for i in range(count)])  12 us
    ppermute x3, starting transfers between devices, program(): lax.ppermute(parts[k], 'head', [(i, (i + 2 * k) % COLS) for i in range(CO...  6.28 us
    ppermute x3, waiting for transfers between devices, program(): lax.ppermute(parts[k], 'head', [(i, (i + 2 * k) % COLS) for i in range(CO...  5.36 us
    ppermute x3, starting transfers between devices, program(): closings.append(lax.ppermute(closing[k], 'seq', route))  4.78 us
  transfers between devices with their start and end apart: 17, of which 9 were waited for; matrix products, arithmetic and copies ran while one was open for 10% of the time, Pallas kernels for 2%

profile of v2, /device:TPU:8, one launch (start us, length us, event | category | flops | bytes accessed | tf_op | source)
XLA Modules:
  0.0 117.3 jit_solution(8889740209613090305)
XLA Ops:
  0.6 15.1 %local.1 = (f32[4,512,128]{2,1,0:T(8,128)}, bf16[4,512,128]{2,1,0:T(8,128)(2,1)}, bf16[4,2,128,128]{3,2,1,0:T(8,128)(2,1)}, bf16[4,5,128,128]{3,2,1,0:T(8,128)(2,1)}, f32[4,4,1,128]{3,2,1,0:T(1,128)}) custom-call(s32[4]{0:T(128)} %refs_0_.1, s32[1]{0:T(128)} %bitcast.1.refs_1_, bf16[512,256]{1,0:T(8,128)(2,1)} %refs_2_.1, bf16[512,256]{1,0:T(8,128)(2,1)} %refs_3_.1, ...), custom_call_target="tpu_custom_call" | custom-call | tf_op jit(solution)/shard_map/local/pallas_call | solution.py:342
  15.7 5.6 %all-to-all-start = ((bf16[4,2,128,128]{3,2,1,0:T(8,128)(2,1)}), bf16[4,2,128,128]{3,2,1,0:T(8,128)(2,1)S(1)}, u32[]{:S(2)}, u32[]{:S(2)}) async-start(bf16[4,2,128,128]{3,2,1,0:T(8,128)(2,1)} %get-tuple-element.12), calls=%async_computation | async-start | bytes 524288 | tf_op jit(solution)/shard_map/all_to_all | solution.py:309
  21.3 1.9 %slice_bitcast_fusion.2 = (bf16[5,128,128]{2,1,0:T(8,128)(2,1)}, bf16[5,128,128]{2,1,0:T(8,128)(2,1)}, bf16[5,128,128]{2,1,0:T(8,128)(2,1)}) fusion(bf16[4,5,128,128]{3,2,1,0:T(8,128)(2,1)} %get-tuple-element.15), kind=kLoop, calls=%fused_computation.33 | loop fusion | bytes 983040 | tf_op jit(solution)/shard_map/squeeze | solution.py:368
  23.1 0.0 copy-start
  23.1 0.0 copy-start.1
  23.1 1.5 %collective-permute-start.10 = (bf16[5,128,128]{2,1,0:T(8,128)(2,1)}, bf16[5,128,128]{2,1,0:T(8,128)(2,1)}, u32[]{:S(2)}, u32[]{:S(2)}) collective-permute-start(bf16[5,128,128]{2,1,0:T(8,128)(2,1)} %get-tuple-element.22), channel_id=1, source_target_pairs={{0,8},{8,16},{16,24},{24,0},{32,40},{40,48},{48,56},{56,32},{64,72... | collective-permute-start | bytes 491528 | tf_op jit(solution)/shard_map/ppermute | solution.py:368
  24.7 0.7 collective-permute-start.9
  25.4 2.5 %collective-permute-start.8 = (bf16[5,128,128]{2,1,0:T(8,128)(2,1)}, bf16[5,128,128]{2,1,0:T(8,128)(2,1)}, u32[]{:S(2)}, u32[]{:S(2)}) collective-permute-start(bf16[5,128,128]{2,1,0:T(8,128)(2,1)} %get-tuple-element.21), channel_id=1, source_target_pairs={{0,24},{8,0},{16,8},{24,16},{32,56},{40,32},{48,40},{56,48},{64,88... | collective-permute-start | bytes 491528 | tf_op jit(solution)/shard_map/ppermute | solution.py:368
  27.9 0.7 fusion.40
  28.6 0.0 all-to-all-done
  28.7 0.1 convolution_add_fusion.3
  28.8 0.2 fusion.41
  29.0 0.1 fusion.1
  29.1 5.9 %collective-permute-start.2 = (bf16[128,256]{1,0:T(8,128)(2,1)S(1)}, bf16[128,256]{1,0:T(8,128)(2,1)S(1)}, u32[]{:S(2)}, u32[]{:S(2)}) collective-permute-start(bf16[128,256]{1,0:T(8,128)(2,1)S(1)} %fusion.1), channel_id=1, source_target_pairs={{0,96},{8,104},{16,112},{24,120},{32,128},{40,136},{48,144},{56,15... | collective-permute-start | bytes 196616 | tf_op jit(solution)/shard_map/ppermute | solution.py:298
  35.0 0.1 fusion.2
  35.1 6.4 %collective-permute-start.3 = (bf16[128,128]{1,0:T(8,128)(2,1)S(1)}, bf16[128,128]{1,0:T(8,128)(2,1)S(1)}, u32[]{:S(2)}, u32[]{:S(2)}) collective-permute-start(bf16[128,128]{1,0:T(8,128)(2,1)S(1)} %fusion.2), channel_id=1, source_target_pairs={{0,128},{8,136},{16,144},{24,152},{32,160},{40,168},{48,176},{56,1... | collective-permute-start | bytes 98312 | tf_op jit(solution)/shard_map/ppermute | solution.py:298
  41.6 1.5 %collective-permute-done.3 = bf16[128,128]{1,0:T(8,128)(2,1)S(1)} collective-permute-done((bf16[128,128]{1,0:T(8,128)(2,1)S(1)}, bf16[128,128]{1,0:T(8,128)(2,1)S(1)}, u32[]{:S(2)}, u32[]{:S(2)}) %collective-permute-start.3) | collective-permute-done | bytes 32800 | tf_op jit(solution)/shard_map/ppermute | solution.py:298
  43.1 1.3 %collective-permute-start = (bf16[128,256]{1,0:T(8,128)(2,1)S(1)}, bf16[128,256]{1,0:T(8,128)(2,1)S(1)}, u32[]{:S(2)}, u32[]{:S(2)}) collective-permute-start(bf16[128,256]{1,0:T(8,128)(2,1)S(1)} %fusion.1), channel_id=1, source_target_pairs={{0,32},{8,40},{16,48},{24,56},{32,64},{40,72},{48,80},{56,88},{64,... | collective-permute-start | bytes 196616 | tf_op jit(solution)/shard_map/ppermute | solution.py:298
  44.4 0.0 collective-permute-done.2
  44.4 2.5 %collective-permute-start.1 = (bf16[128,256]{1,0:T(8,128)(2,1)S(1)}, bf16[128,256]{1,0:T(8,128)(2,1)S(1)}, u32[]{:S(2)}, u32[]{:S(2)}) collective-permute-start(bf16[128,256]{1,0:T(8,128)(2,1)S(1)} %fusion.1), channel_id=1, source_target_pairs={{0,64},{8,72},{16,80},{24,88},{32,96},{40,104},{48,112},{56,120},{... | collective-permute-start | bytes 196616 | tf_op jit(solution)/shard_map/ppermute | solution.py:298
  46.9 0.1 fusion.27
  47.0 0.0 collective-permute-done
  47.0 1.8 %collective-permute-done.1 = bf16[128,256]{1,0:T(8,128)(2,1)S(1)} collective-permute-done((bf16[128,256]{1,0:T(8,128)(2,1)S(1)}, bf16[128,256]{1,0:T(8,128)(2,1)S(1)}, u32[]{:S(2)}, u32[]{:S(2)}) %collective-permute-start.1) | collective-permute-done | bytes 65568 | tf_op jit(solution)/shard_map/ppermute | solution.py:298
  48.8 0.3 add_convert_fusion.3
  49.0 0.2 fusion
  49.2 0.8 fusion.15
  50.0 4.8 %all-to-all-start.1 = ((bf16[4,128,128]{2,1,0:T(8,128)(2,1)}), bf16[4,128,128]{2,1,0:T(8,128)(2,1)S(1)}, u32[]{:S(2)}, u32[]{:S(2)}) async-start(bf16[4,128,128]{2,1,0:T(8,128)(2,1)} %get-tuple-element.32), calls=%async_computation.1 | async-start | bytes 262144 | tf_op jit(solution)/shard_map/all_to_all | solution.py:309
  54.7 0.9 fusion.25
  55.6 3.6 %all-to-all-done.1.arriving_ref = bf16[4,128,128]{2,1,0:T(8,128)(2,1)S(1)} async-done(((bf16[4,128,128]{2,1,0:T(8,128)(2,1)}), bf16[4,128,128]{2,1,0:T(8,128)(2,1)S(1)}, u32[]{:S(2)}, u32[]{:S(2)}) %all-to-all-start.1) | async-done | bytes 131104 | tf_op jit(solution)/shard_map/all_to_all | solution.py:309
  59.2 0.0 copy-done
  59.3 0.0 copy-done.1
  59.3 0.0 copy-done.2
  59.3 2.6 %send.1 = (bf16[512,512]{1,0:T(8,128)(2,1)S(1)}, bf16[4,512,256]{2,1,0:T(8,128)(2,1)S(1)}) custom-call(s32[1]{0:T(128)} %bitcast.place_ref, f32[4,512,128]{2,1,0:T(8,128)S(1)} %copy-done, bf16[4,512,128]{2,1,0:T(8,128)(2,1)S(1)} %copy-done.1, bf16[4,128,128]{2,1,0:T(8,128)(2,1)S(1)} %all-to-all-done.1.arriving_ref, f32[1,128]{1,0:T(1,128)S(1)} %bitcast.96, ...), custom_call_target="tpu_custom_call" | custom-call | tf_op jit(solution)/shard_map/send/pallas_call | solution.py:405
  61.9 0.1 collective-permute-start.4
  62.0 0.0 collective-permute-done.10
  62.0 0.9 fusion.22
  62.9 0.0 collective-permute-done.9
  62.9 0.9 fusion.23
  63.8 0.0 collective-permute-done.8
  63.8 0.9 fusion.24
  64.7 1.3 %fusion.12 = bf16[4,128,128]{2,1,0:T(8,128)(2,1)S(1)} fusion(bf16[5,128,128]{2,1,0:T(8,128)(2,1)} %collective-permute-done.10, bf16[5,128,128]{2,1,0:T(8,128)(2,1)} %collective-permute-done.9, bf16[5,128,128]{2,1,0:T(8,128)(2,1)} %collective-permute-done.8, f32[128,128]{1,0:T(8,128)S(1)} %fusion.22, f32[4,128]{1,0:T(4,128)S(1)} %bitcast.101, ...), kind=kLoop, calls=%fused_computation.28 | loop fusion | flops 1048576 | bytes 925696 | tf_op jit(solution)/shard_map/convert_element_type | solution.py:397
  66.0 11.0 %collective-permute-start.11 = (bf16[4,128,128]{2,1,0:T(8,128)(2,1)S(1)}, bf16[4,128,128]{2,1,0:T(8,128)(2,1)S(1)}, u32[]{:S(2)}, u32[]{:S(2)}) collective-permute-start(bf16[4,128,128]{2,1,0:T(8,128)(2,1)S(1)} %fusion.12), channel_id=1, source_target_pairs={{0,128},{8,136},{16,144},{24,152},{32,160},{40,168},{48,176},{56,1... | collective-permute-start | bytes 393224 | tf_op jit(solution)/shard_map/ppermute | solution.py:303
  77.0 2.3 %keep.1 = bf16[4,512,256]{2,1,0:T(8,128)(2,1)S(1)} custom-call(s32[1]{0:T(128)} %bitcast.place_ref, bf16[512,512]{1,0:T(8,128)(2,1)S(1)} %get-tuple-element.13.hidden_ref, bf16[512,2048]{1,0:T(8,128)(2,1)} %weight_ref.3), custom_call_target="tpu_custom_call" | custom-call | tf_op jit(solution)/shard_map/keep/pallas_call | solution.py:417
  79.3 0.0 copy-start.3
  79.3 4.7 %collective-permute-done.11 = bf16[4,128,128]{2,1,0:T(8,128)(2,1)S(1)} collective-permute-done((bf16[4,128,128]{2,1,0:T(8,128)(2,1)S(1)}, bf16[4,128,128]{2,1,0:T(8,128)(2,1)S(1)}, u32[]{:S(2)}, u32[]{:S(2)}) %collective-permute-start.11) | collective-permute-done | bytes 131104 | tf_op jit(solution)/shard_map/ppermute | solution.py:303
  84.0 0.7 collective-permute-start.12
  84.7 0.0 collective-permute-done.4
  84.7 1.3 %fusion.6 = (bf16[512,256]{1,0:T(8,128)(2,1)S(1)}, bf16[512,256]{1,0:T(8,128)(2,1)S(1)}, bf16[512,256]{1,0:T(8,128)(2,1)S(1)}) fusion(bf16[4,512,256]{2,1,0:T(8,128)(2,1)} %collective-permute-done.4, bf16[4,512,256]{2,1,0:T(8,128)(2,1)S(1)} %keep.1), kind=kLoop, calls=%fused_computation.17 | loop fusion | flops 1572864 | bytes 2359296 | tf_op jit(solution)/shard_map/convert_element_type | solution.py:426
  86.0 6.4 %collective-permute-done.12 = bf16[4,128,128]{2,1,0:T(8,128)(2,1)S(1)} collective-permute-done((bf16[4,128,128]{2,1,0:T(8,128)(2,1)S(1)}, bf16[4,128,128]{2,1,0:T(8,128)(2,1)S(1)}, u32[]{:S(2)}, u32[]{:S(2)}) %collective-permute-start.12) | collective-permute-done | bytes 131104 | tf_op jit(solution)/shard_map/ppermute | solution.py:303
  92.5 0.3 collective-permute-start.13
  92.8 0.0 copy-done.3
  92.8 0.1 broadcast_compare_fusion
  92.9 4.7 %collective-permute-done.13 = bf16[4,128,128]{2,1,0:T(8,128)(2,1)S(1)} collective-permute-done((bf16[4,128,128]{2,1,0:T(8,128)(2,1)S(1)}, bf16[4,128,128]{2,1,0:T(8,128)(2,1)S(1)}, u32[]{:S(2)}, u32[]{:S(2)}) %collective-permute-start.13) | collective-permute-done | bytes 131104 | tf_op jit(solution)/shard_map/ppermute | solution.py:303
  97.6 0.8 select_reduce_fusion
  98.4 4.8 %all-to-all-start.2 = ((bf16[4,128,128]{2,1,0:T(8,128)(2,1)}), bf16[4,128,128]{2,1,0:T(8,128)(2,1)S(1)}, u32[]{:S(2)}, u32[]{:S(2)}) async-start(bf16[4,128,128]{2,1,0:T(8,128)(2,1)} %select_reduce_fusion), calls=%async_computation.2 | async-start | bytes 262144 | tf_op jit(solution)/shard_map/all_to_all | solution.py:309
  103.2 3.0 %collective-permute-start.5 = (bf16[512,256]{1,0:T(8,128)(2,1)S(1)}, bf16[512,256]{1,0:T(8,128)(2,1)S(1)}, u32[]{:S(2)}, u32[]{:S(2)}) collective-permute-start(bf16[512,256]{1,0:T(8,128)(2,1)S(1)} %get-tuple-element.18), channel_id=1, source_target_pairs={{0,4},{1,5},{2,6},{3,7},{4,0},{5,1},{6,2},{7,3},{8,12},{9,13},{10,... | collective-permute-start | bytes 786440 | tf_op jit(solution)/shard_map/ppermute | solution.py:438
  106.2 0.6 collective-permute-start.6
  106.8 2.7 %collective-permute-start.7 = (bf16[512,256]{1,0:T(8,128)(2,1)S(1)}, bf16[512,256]{1,0:T(8,128)(2,1)S(1)}, u32[]{:S(2)}, u32[]{:S(2)}) collective-permute-start(bf16[512,256]{1,0:T(8,128)(2,1)S(1)} %get-tuple-element.19), channel_id=1, source_target_pairs={{0,6},{1,7},{2,0},{3,1},{4,2},{5,3},{6,4},{7,5},{8,14},{9,15},{10,... | collective-permute-start | bytes 786440 | tf_op jit(solution)/shard_map/ppermute | solution.py:438
  109.4 0.0 all-to-all-done.2
  109.4 0.7 bitcast_convert_fusion
  110.2 2.6 %collective-permute-done.5 = bf16[512,256]{1,0:T(8,128)(2,1)S(1)} collective-permute-done((bf16[512,256]{1,0:T(8,128)(2,1)S(1)}, bf16[512,256]{1,0:T(8,128)(2,1)S(1)}, u32[]{:S(2)}, u32[]{:S(2)}) %collective-permute-start.5) | collective-permute-done | bytes 262176 | tf_op jit(solution)/shard_map/ppermute | solution.py:438
  112.7 2.7 %collective-permute-done.6 = bf16[512,256]{1,0:T(8,128)(2,1)S(1)} collective-permute-done((bf16[512,256]{1,0:T(8,128)(2,1)S(1)}, bf16[512,256]{1,0:T(8,128)(2,1)S(1)}, u32[]{:S(2)}, u32[]{:S(2)}) %collective-permute-start.6) | collective-permute-done | bytes 262176 | tf_op jit(solution)/shard_map/ppermute | solution.py:438
  115.4 0.1 collective-permute-done.7
  115.5 1.8 %fusion.5 = bf16[512,256]{1,0:T(8,128)(2,1)} fusion(bf16[512,256]{1,0:T(8,128)(2,1)S(1)} %collective-permute-done.7, bf16[512,256]{1,0:T(8,128)(2,1)S(1)} %collective-permute-done.6, bf16[512,256]{1,0:T(8,128)(2,1)S(1)} %collective-permute-done.5, bf16[4,512,256]{2,1,0:T(8,128)(2,1)} %collective-permute-done.4, bf16[4,512,256]{2,1,0:T(8,128)(2,1)S(1)} %keep.1), kind=kLoop, calls=%fused_computation.12 | loop fusion | flops 1310720 | bytes 1572864 | tf_op jit(solution)/shard_map/convert_element_type | solution.py:442
  (8 shorter events, 0.2 us)
Async XLA Ops:
  15.7 12.9 %all-to-all-start = ((bf16[4,2,128,128]{3,2,1,0:T(8,128)(2,1)}), bf16[4,2,128,128]{3,2,1,0:T(8,128)(2,1)S(1)}, u32[]{:S(2)}, u32[]{:S(2)}) async-start(bf16[4,2,128,128]{3,2,1,0:T(8,128)(2,1)} %get-tuple-element.12), calls=%async_computation | async-start | bytes 524288 | tf_op jit(solution)/shard_map/all_to_all | solution.py:309
  23.1 36.1 %copy-start = (f32[4,512,128]{2,1,0:T(8,128)S(1)}, f32[4,512,128]{2,1,0:T(8,128)}, u32[]{:S(2)}) copy-start(f32[4,512,128]{2,1,0:T(8,128)} %get-tuple-element.10.out_ref) | copy-start | bytes 3145732
  23.1 36.1 %copy-start.1 = (bf16[4,512,128]{2,1,0:T(8,128)(2,1)S(1)}, bf16[4,512,128]{2,1,0:T(8,128)(2,1)}, u32[]{:S(2)}) copy-start(bf16[4,512,128]{2,1,0:T(8,128)(2,1)} %get-tuple-element.11.link_ref) | copy-start | bytes 1572868
  23.1 36.1 %copy-start.2 = (f32[128]{0:T(128)S(1)}, f32[128]{0:T(128)}, u32[]{:S(2)}) copy-start(f32[128]{0:T(128)} %param.16) | copy-start | bytes 1540
  23.1 38.9 %collective-permute-start.10 = (bf16[5,128,128]{2,1,0:T(8,128)(2,1)}, bf16[5,128,128]{2,1,0:T(8,128)(2,1)}, u32[]{:S(2)}, u32[]{:S(2)}) collective-permute-start(bf16[5,128,128]{2,1,0:T(8,128)(2,1)} %get-tuple-element.22), channel_id=1, source_target_pairs={{0,8},{8,16},{16,24},{24,0},{32,40},{40,48},{48,56},{56,32},{64,72... | collective-permute-start | bytes 491528 | tf_op jit(solution)/shard_map/ppermute | solution.py:368
  24.7 38.2 %collective-permute-start.9 = (bf16[5,128,128]{2,1,0:T(8,128)(2,1)}, bf16[5,128,128]{2,1,0:T(8,128)(2,1)}, u32[]{:S(2)}, u32[]{:S(2)}) collective-permute-start(bf16[5,128,128]{2,1,0:T(8,128)(2,1)} %get-tuple-element.23), channel_id=1, source_target_pairs={{0,16},{8,24},{16,0},{24,8},{32,48},{40,56},{48,32},{56,40},{64,80... | collective-permute-start | bytes 491528 | tf_op jit(solution)/shard_map/ppermute | solution.py:368
  25.4 38.4 %collective-permute-start.8 = (bf16[5,128,128]{2,1,0:T(8,128)(2,1)}, bf16[5,128,128]{2,1,0:T(8,128)(2,1)}, u32[]{:S(2)}, u32[]{:S(2)}) collective-permute-start(bf16[5,128,128]{2,1,0:T(8,128)(2,1)} %get-tuple-element.21), channel_id=1, source_target_pairs={{0,24},{8,0},{16,8},{24,16},{32,56},{40,32},{48,40},{56,48},{64,88... | collective-permute-start | bytes 491528 | tf_op jit(solution)/shard_map/ppermute | solution.py:368
  29.1 15.3 %collective-permute-start.2 = (bf16[128,256]{1,0:T(8,128)(2,1)S(1)}, bf16[128,256]{1,0:T(8,128)(2,1)S(1)}, u32[]{:S(2)}, u32[]{:S(2)}) collective-permute-start(bf16[128,256]{1,0:T(8,128)(2,1)S(1)} %fusion.1), channel_id=1, source_target_pairs={{0,96},{8,104},{16,112},{24,120},{32,128},{40,136},{48,144},{56,15... | collective-permute-start | bytes 196616 | tf_op jit(solution)/shard_map/ppermute | solution.py:298
  35.1 8.0 %collective-permute-start.3 = (bf16[128,128]{1,0:T(8,128)(2,1)S(1)}, bf16[128,128]{1,0:T(8,128)(2,1)S(1)}, u32[]{:S(2)}, u32[]{:S(2)}) collective-permute-start(bf16[128,128]{1,0:T(8,128)(2,1)S(1)} %fusion.2), channel_id=1, source_target_pairs={{0,128},{8,136},{16,144},{24,152},{32,160},{40,168},{48,176},{56,1... | collective-permute-start | bytes 98312 | tf_op jit(solution)/shard_map/ppermute | solution.py:298
  43.1 3.9 %collective-permute-start = (bf16[128,256]{1,0:T(8,128)(2,1)S(1)}, bf16[128,256]{1,0:T(8,128)(2,1)S(1)}, u32[]{:S(2)}, u32[]{:S(2)}) collective-permute-start(bf16[128,256]{1,0:T(8,128)(2,1)S(1)} %fusion.1), channel_id=1, source_target_pairs={{0,32},{8,40},{16,48},{24,56},{32,64},{40,72},{48,80},{56,88},{64,... | collective-permute-start | bytes 196616 | tf_op jit(solution)/shard_map/ppermute | solution.py:298
  44.4 4.3 %collective-permute-start.1 = (bf16[128,256]{1,0:T(8,128)(2,1)S(1)}, bf16[128,256]{1,0:T(8,128)(2,1)S(1)}, u32[]{:S(2)}, u32[]{:S(2)}) collective-permute-start(bf16[128,256]{1,0:T(8,128)(2,1)S(1)} %fusion.1), channel_id=1, source_target_pairs={{0,64},{8,72},{16,80},{24,88},{32,96},{40,104},{48,112},{56,120},{... | collective-permute-start | bytes 196616 | tf_op jit(solution)/shard_map/ppermute | solution.py:298
  50.0 9.3 %all-to-all-start.1 = ((bf16[4,128,128]{2,1,0:T(8,128)(2,1)}), bf16[4,128,128]{2,1,0:T(8,128)(2,1)S(1)}, u32[]{:S(2)}, u32[]{:S(2)}) async-start(bf16[4,128,128]{2,1,0:T(8,128)(2,1)} %get-tuple-element.32), calls=%async_computation.1 | async-start | bytes 262144 | tf_op jit(solution)/shard_map/all_to_all | solution.py:309
  61.9 22.8 %collective-permute-start.4 = (bf16[4,512,256]{2,1,0:T(8,128)(2,1)S(1)}, bf16[4,512,256]{2,1,0:T(8,128)(2,1)}, u32[]{:S(2)}, u32[]{:S(2)}) collective-permute-start(bf16[4,512,256]{2,1,0:T(8,128)(2,1)S(1)} %get-tuple-element.14), channel_id=1, source_target_pairs={{0,1},{1,0},{2,3},{3,2},{4,5},{5,4},{6,7},{7,6},{8,9},{9,8},{10,11... | collective-permute-start | bytes 3145736 | tf_op jit(solution)/shard_map/ppermute | solution.py:416
  66.0 18.0 %collective-permute-start.11 = (bf16[4,128,128]{2,1,0:T(8,128)(2,1)S(1)}, bf16[4,128,128]{2,1,0:T(8,128)(2,1)S(1)}, u32[]{:S(2)}, u32[]{:S(2)}) collective-permute-start(bf16[4,128,128]{2,1,0:T(8,128)(2,1)S(1)} %fusion.12), channel_id=1, source_target_pairs={{0,128},{8,136},{16,144},{24,152},{32,160},{40,168},{48,176},{56,1... | collective-permute-start | bytes 393224 | tf_op jit(solution)/shard_map/ppermute | solution.py:303
  79.3 13.5 %copy-start.3 = (s32[4]{0:T(128)S(1)}, s32[4]{0:T(128)}, u32[]{:S(2)}) copy-start(s32[4]{0:T(128)} %param.15) | copy-start | bytes 52
  84.0 8.4 %collective-permute-start.12 = (bf16[4,128,128]{2,1,0:T(8,128)(2,1)S(1)}, bf16[4,128,128]{2,1,0:T(8,128)(2,1)S(1)}, u32[]{:S(2)}, u32[]{:S(2)}) collective-permute-start(bf16[4,128,128]{2,1,0:T(8,128)(2,1)S(1)} %add.132), channel_id=1, source_target_pairs={{0,64},{8,72},{16,80},{24,88},{32,96},{40,104},{48,112},{56,120},{... | collective-permute-start | bytes 393224 | tf_op jit(solution)/shard_map/ppermute | solution.py:303
  92.5 5.1 %collective-permute-start.13 = (bf16[4,128,128]{2,1,0:T(8,128)(2,1)S(1)}, bf16[4,128,128]{2,1,0:T(8,128)(2,1)S(1)}, u32[]{:S(2)}, u32[]{:S(2)}) collective-permute-start(bf16[4,128,128]{2,1,0:T(8,128)(2,1)S(1)} %add.133), channel_id=1, source_target_pairs={{0,32},{8,40},{16,48},{24,56},{32,0},{40,8},{48,16},{56,24},{64,96... | collective-permute-start | bytes 393224 | tf_op jit(solution)/shard_map/ppermute | solution.py:303
  98.4 11.0 %all-to-all-start.2 = ((bf16[4,128,128]{2,1,0:T(8,128)(2,1)}), bf16[4,128,128]{2,1,0:T(8,128)(2,1)S(1)}, u32[]{:S(2)}, u32[]{:S(2)}) async-start(bf16[4,128,128]{2,1,0:T(8,128)(2,1)} %select_reduce_fusion), calls=%async_computation.2 | async-start | bytes 262144 | tf_op jit(solution)/shard_map/all_to_all | solution.py:309
  103.2 9.6 %collective-permute-start.5 = (bf16[512,256]{1,0:T(8,128)(2,1)S(1)}, bf16[512,256]{1,0:T(8,128)(2,1)S(1)}, u32[]{:S(2)}, u32[]{:S(2)}) collective-permute-start(bf16[512,256]{1,0:T(8,128)(2,1)S(1)} %get-tuple-element.18), channel_id=1, source_target_pairs={{0,4},{1,5},{2,6},{3,7},{4,0},{5,1},{6,2},{7,3},{8,12},{9,13},{10,... | collective-permute-start | bytes 786440 | tf_op jit(solution)/shard_map/ppermute | solution.py:438
  106.2 9.2 %collective-permute-start.6 = (bf16[512,256]{1,0:T(8,128)(2,1)S(1)}, bf16[512,256]{1,0:T(8,128)(2,1)S(1)}, u32[]{:S(2)}, u32[]{:S(2)}) collective-permute-start(bf16[512,256]{1,0:T(8,128)(2,1)S(1)} %get-tuple-element.20), channel_id=1, source_target_pairs={{0,2},{1,3},{2,4},{3,5},{4,6},{5,7},{6,0},{7,1},{8,10},{9,11},{10,... | collective-permute-start | bytes 786440 | tf_op jit(solution)/shard_map/ppermute | solution.py:438
  106.8 8.8 %collective-permute-start.7 = (bf16[512,256]{1,0:T(8,128)(2,1)S(1)}, bf16[512,256]{1,0:T(8,128)(2,1)S(1)}, u32[]{:S(2)}, u32[]{:S(2)}) collective-permute-start(bf16[512,256]{1,0:T(8,128)(2,1)S(1)} %get-tuple-element.19), channel_id=1, source_target_pairs={{0,6},{1,7},{2,0},{3,1},{4,2},{5,3},{6,4},{7,5},{8,14},{9,15},{10,... | collective-permute-start | bytes 786440 | tf_op jit(solution)/shard_map/ppermute | solution.py:438

commit v3 on v2

--- a/solution.py
+++ b/solution.py
@@ -391,9 +391,9 @@
     turned = lax.dynamic_slice_in_dim(
         jnp.concatenate([starts, starts]), position % ROWS, ROWS, axis=0
     )
+    carried = [dot(closings[k][4], turned[k])[None] for k in range(ROWS)]
     finals = sum(
-        closings[k][:4].astype(F32) + flags[k] * dot(closings[k][4], turned[k])[None]
-        for k in range(ROWS)
+        closings[k][:4].astype(F32) + flags[k] * carried[k] for k in range(ROWS)
     ).astype(BF16)
 
     other = swapped(finals, 4 * ROWS)
@@ -433,13 +433,18 @@
     parcels = jnp.sum(jnp.where(chosen, finals[None], 0.0), axis=1).astype(BF16)
     owned = traded(parcels).astype(F32)
 
+    moved = []
+    for k in (2, 1, 3):
+        moved.append(
+            lax.ppermute(
+                parts[k], "head", [(i, (i + 2 * k) % COLS) for i in range(COLS)]
+            )
+        )
     mixed = sums[0]
-    for k in (2, 1, 3):
-        moved = lax.ppermute(
-            parts[k], "head", [(i, (i + 2 * k) % COLS) for i in range(COLS)]
-        )
-        mixed = mixed + moved.astype(F32)
-    return (mixed.astype(BF16), owned[None])
+    for part in moved:
+        mixed = mixed + part.astype(F32)
+    mixed = mixed.astype(BF16)
+    return (mixed, owned[None])
 
 
 def solution(mesh):

time: 119 us -> 119 us (level)
  no operation moved by 1% of the time
where the time goes in v3:
time: 119 us; the launch traced here: 117 us
  starting transfers between devices  54.3 us (46%)
  waiting for transfers between devices  28.1 us (24%)
  Pallas kernels  20 us (17%)
  other arithmetic  6.89 us (6%)
  matrix products  4.71 us (4%)
  local copies, waits for them, and re-layouts  2.57 us (2%)
    ppermute x4, starting transfers between devices, shifted(): lax.ppermute(block, 'seq', [(i, i + distance) for i in range(count - dist...  16 us
    ppermute x3, waiting for transfers between devices, swapped(): return lax.ppermute(block, 'seq', [(i, i ^ distance) for i in range(count)])  15.8 us
    all_to_all x3, starting transfers between devices, traded(): return lax.all_to_all(blocks, 'seq', 0, 0, axis_index_groups=groups)  15.1 us
    pallas_call x1, Pallas kernels, program(): pl.pallas_call(kernel, out_shape=(jax.ShapeDtypeStruct((4, local_rows, DV...  15.1 us
    ppermute x3, starting transfers between devices, swapped(): return lax.ppermute(block, 'seq', [(i, i ^ distance) for i in range(count)])  12 us
    ppermute x3, starting transfers between devices, program(): lax.ppermute(parts[k], 'head', [(i, (i + 2 * k) % COLS) for i in range(CO...  6.28 us
    ppermute x3, waiting for transfers between devices, program(): lax.ppermute(parts[k], 'head', [(i, (i + 2 * k) % COLS) for i in range(CO...  5.36 us
    ppermute x3, starting transfers between devices, program(): closings.append(lax.ppermute(closing[k], 'seq', route))  4.78 us
  transfers between devices with their start and end apart: 17, of which 9 were waited for; matrix products, arithmetic and copies ran while one was open for 10% of the time, Pallas kernels for 2%

profile of v3, /device:TPU:8, one launch (start us, length us, event | category | flops | bytes accessed | tf_op | source)
XLA Modules:
  0.0 117.3 jit_solution(8889740209613090305)
XLA Ops:
  0.6 15.1 %local.1 = (f32[4,512,128]{2,1,0:T(8,128)}, bf16[4,512,128]{2,1,0:T(8,128)(2,1)}, bf16[4,2,128,128]{3,2,1,0:T(8,128)(2,1)}, bf16[4,5,128,128]{3,2,1,0:T(8,128)(2,1)}, f32[4,4,1,128]{3,2,1,0:T(1,128)}) custom-call(s32[4]{0:T(128)} %refs_0_.1, s32[1]{0:T(128)} %bitcast.1.refs_1_, bf16[512,256]{1,0:T(8,128)(2,1)} %refs_2_.1, bf16[512,256]{1,0:T(8,128)(2,1)} %refs_3_.1, ...), custom_call_target="tpu_custom_call" | custom-call | tf_op jit(solution)/shard_map/local/pallas_call | solution.py:342
  15.7 5.6 %all-to-all-start = ((bf16[4,2,128,128]{3,2,1,0:T(8,128)(2,1)}), bf16[4,2,128,128]{3,2,1,0:T(8,128)(2,1)S(1)}, u32[]{:S(2)}, u32[]{:S(2)}) async-start(bf16[4,2,128,128]{3,2,1,0:T(8,128)(2,1)} %get-tuple-element.12), calls=%async_computation | async-start | bytes 524288 | tf_op jit(solution)/shard_map/all_to_all | solution.py:309
  21.3 1.9 %slice_bitcast_fusion.2 = (bf16[5,128,128]{2,1,0:T(8,128)(2,1)}, bf16[5,128,128]{2,1,0:T(8,128)(2,1)}, bf16[5,128,128]{2,1,0:T(8,128)(2,1)}) fusion(bf16[4,5,128,128]{3,2,1,0:T(8,128)(2,1)} %get-tuple-element.15), kind=kLoop, calls=%fused_computation.33 | loop fusion | bytes 983040 | tf_op jit(solution)/shard_map/squeeze | solution.py:368
  23.1 0.0 copy-start
  23.1 0.0 copy-start.1
  23.1 1.5 %collective-permute-start.10 = (bf16[5,128,128]{2,1,0:T(8,128)(2,1)}, bf16[5,128,128]{2,1,0:T(8,128)(2,1)}, u32[]{:S(2)}, u32[]{:S(2)}) collective-permute-start(bf16[5,128,128]{2,1,0:T(8,128)(2,1)} %get-tuple-element.22), channel_id=1, source_target_pairs={{0,8},{8,16},{16,24},{24,0},{32,40},{40,48},{48,56},{56,32},{64,72... | collective-permute-start | bytes 491528 | tf_op jit(solution)/shard_map/ppermute | solution.py:368
  24.7 0.7 collective-permute-start.9
  25.4 2.5 %collective-permute-start.8 = (bf16[5,128,128]{2,1,0:T(8,128)(2,1)}, bf16[5,128,128]{2,1,0:T(8,128)(2,1)}, u32[]{:S(2)}, u32[]{:S(2)}) collective-permute-start(bf16[5,128,128]{2,1,0:T(8,128)(2,1)} %get-tuple-element.21), channel_id=1, source_target_pairs={{0,24},{8,0},{16,8},{24,16},{32,56},{40,32},{48,40},{56,48},{64,88... | collective-permute-start | bytes 491528 | tf_op jit(solution)/shard_map/ppermute | solution.py:368
  27.9 0.7 fusion.40
  28.6 0.0 all-to-all-done
  28.7 0.1 convolution_add_fusion.3
  28.8 0.2 fusion.41
  29.0 0.1 fusion.1
  29.1 5.9 %collective-permute-start.2 = (bf16[128,256]{1,0:T(8,128)(2,1)S(1)}, bf16[128,256]{1,0:T(8,128)(2,1)S(1)}, u32[]{:S(2)}, u32[]{:S(2)}) collective-permute-start(bf16[128,256]{1,0:T(8,128)(2,1)S(1)} %fusion.1), channel_id=1, source_target_pairs={{0,96},{8,104},{16,112},{24,120},{32,128},{40,136},{48,144},{56,15... | collective-permute-start | bytes 196616 | tf_op jit(solution)/shard_map/ppermute | solution.py:298
  35.0 0.1 fusion.2
  35.1 6.4 %collective-permute-start.3 = (bf16[128,128]{1,0:T(8,128)(2,1)S(1)}, bf16[128,128]{1,0:T(8,128)(2,1)S(1)}, u32[]{:S(2)}, u32[]{:S(2)}) collective-permute-start(bf16[128,128]{1,0:T(8,128)(2,1)S(1)} %fusion.2), channel_id=1, source_target_pairs={{0,128},{8,136},{16,144},{24,152},{32,160},{40,168},{48,176},{56,1... | collective-permute-start | bytes 98312 | tf_op jit(solution)/shard_map/ppermute | solution.py:298
  41.6 1.5 %collective-permute-done.3 = bf16[128,128]{1,0:T(8,128)(2,1)S(1)} collective-permute-done((bf16[128,128]{1,0:T(8,128)(2,1)S(1)}, bf16[128,128]{1,0:T(8,128)(2,1)S(1)}, u32[]{:S(2)}, u32[]{:S(2)}) %collective-permute-start.3) | collective-permute-done | bytes 32800 | tf_op jit(solution)/shard_map/ppermute | solution.py:298
  43.1 1.3 %collective-permute-start = (bf16[128,256]{1,0:T(8,128)(2,1)S(1)}, bf16[128,256]{1,0:T(8,128)(2,1)S(1)}, u32[]{:S(2)}, u32[]{:S(2)}) collective-permute-start(bf16[128,256]{1,0:T(8,128)(2,1)S(1)} %fusion.1), channel_id=1, source_target_pairs={{0,32},{8,40},{16,48},{24,56},{32,64},{40,72},{48,80},{56,88},{64,... | collective-permute-start | bytes 196616 | tf_op jit(solution)/shard_map/ppermute | solution.py:298
  44.4 0.0 collective-permute-done.2
  44.4 2.5 %collective-permute-start.1 = (bf16[128,256]{1,0:T(8,128)(2,1)S(1)}, bf16[128,256]{1,0:T(8,128)(2,1)S(1)}, u32[]{:S(2)}, u32[]{:S(2)}) collective-permute-start(bf16[128,256]{1,0:T(8,128)(2,1)S(1)} %fusion.1), channel_id=1, source_target_pairs={{0,64},{8,72},{16,80},{24,88},{32,96},{40,104},{48,112},{56,120},{... | collective-permute-start | bytes 196616 | tf_op jit(solution)/shard_map/ppermute | solution.py:298
  46.9 0.1 fusion.27
  47.0 0.0 collective-permute-done
  47.0 1.8 %collective-permute-done.1 = bf16[128,256]{1,0:T(8,128)(2,1)S(1)} collective-permute-done((bf16[128,256]{1,0:T(8,128)(2,1)S(1)}, bf16[128,256]{1,0:T(8,128)(2,1)S(1)}, u32[]{:S(2)}, u32[]{:S(2)}) %collective-permute-start.1) | collective-permute-done | bytes 65568 | tf_op jit(solution)/shard_map/ppermute | solution.py:298
  48.8 0.3 add_convert_fusion.3
  49.0 0.2 fusion
  49.2 0.8 fusion.15
  50.0 4.8 %all-to-all-start.1 = ((bf16[4,128,128]{2,1,0:T(8,128)(2,1)}), bf16[4,128,128]{2,1,0:T(8,128)(2,1)S(1)}, u32[]{:S(2)}, u32[]{:S(2)}) async-start(bf16[4,128,128]{2,1,0:T(8,128)(2,1)} %get-tuple-element.32), calls=%async_computation.1 | async-start | bytes 262144 | tf_op jit(solution)/shard_map/all_to_all | solution.py:309
  54.7 0.9 fusion.25
  55.6 3.6 %all-to-all-done.1.arriving_ref = bf16[4,128,128]{2,1,0:T(8,128)(2,1)S(1)} async-done(((bf16[4,128,128]{2,1,0:T(8,128)(2,1)}), bf16[4,128,128]{2,1,0:T(8,128)(2,1)S(1)}, u32[]{:S(2)}, u32[]{:S(2)}) %all-to-all-start.1) | async-done | bytes 131104 | tf_op jit(solution)/shard_map/all_to_all | solution.py:309
  59.2 0.0 copy-done
  59.3 0.0 copy-done.1
  59.3 0.0 copy-done.2
  59.3 2.6 %send.1 = (bf16[512,512]{1,0:T(8,128)(2,1)S(1)}, bf16[4,512,256]{2,1,0:T(8,128)(2,1)S(1)}) custom-call(s32[1]{0:T(128)} %bitcast.place_ref, f32[4,512,128]{2,1,0:T(8,128)S(1)} %copy-done, bf16[4,512,128]{2,1,0:T(8,128)(2,1)S(1)} %copy-done.1, bf16[4,128,128]{2,1,0:T(8,128)(2,1)S(1)} %all-to-all-done.1.arriving_ref, f32[1,128]{1,0:T(1,128)S(1)} %bitcast.96, ...), custom_call_target="tpu_custom_call" | custom-call | tf_op jit(solution)/shard_map/send/pallas_call | solution.py:405
  61.9 0.1 collective-permute-start.4
  62.0 0.0 collective-permute-done.10
  62.0 0.9 fusion.22
  62.9 0.0 collective-permute-done.9
  62.9 0.9 fusion.23
  63.8 0.0 collective-permute-done.8
  63.8 0.9 fusion.24
  64.7 1.3 %fusion.12 = bf16[4,128,128]{2,1,0:T(8,128)(2,1)S(1)} fusion(bf16[5,128,128]{2,1,0:T(8,128)(2,1)} %collective-permute-done.10, bf16[5,128,128]{2,1,0:T(8,128)(2,1)} %collective-permute-done.9, bf16[5,128,128]{2,1,0:T(8,128)(2,1)} %collective-permute-done.8, f32[128,128]{1,0:T(8,128)S(1)} %fusion.22, f32[4,128]{1,0:T(4,128)S(1)} %bitcast.101, ...), kind=kLoop, calls=%fused_computation.28 | loop fusion | flops 1048576 | bytes 925696 | tf_op jit(solution)/shard_map/convert_element_type | solution.py:397
  66.0 11.0 %collective-permute-start.11 = (bf16[4,128,128]{2,1,0:T(8,128)(2,1)S(1)}, bf16[4,128,128]{2,1,0:T(8,128)(2,1)S(1)}, u32[]{:S(2)}, u32[]{:S(2)}) collective-permute-start(bf16[4,128,128]{2,1,0:T(8,128)(2,1)S(1)} %fusion.12), channel_id=1, source_target_pairs={{0,128},{8,136},{16,144},{24,152},{32,160},{40,168},{48,176},{56,1... | collective-permute-start | bytes 393224 | tf_op jit(solution)/shard_map/ppermute | solution.py:303
  77.0 2.3 %keep.1 = bf16[4,512,256]{2,1,0:T(8,128)(2,1)S(1)} custom-call(s32[1]{0:T(128)} %bitcast.place_ref, bf16[512,512]{1,0:T(8,128)(2,1)S(1)} %get-tuple-element.13.hidden_ref, bf16[512,2048]{1,0:T(8,128)(2,1)} %weight_ref.3), custom_call_target="tpu_custom_call" | custom-call | tf_op jit(solution)/shard_map/keep/pallas_call | solution.py:417
  79.3 0.0 copy-start.3
  79.3 4.7 %collective-permute-done.11 = bf16[4,128,128]{2,1,0:T(8,128)(2,1)S(1)} collective-permute-done((bf16[4,128,128]{2,1,0:T(8,128)(2,1)S(1)}, bf16[4,128,128]{2,1,0:T(8,128)(2,1)S(1)}, u32[]{:S(2)}, u32[]{:S(2)}) %collective-permute-start.11) | collective-permute-done | bytes 131104 | tf_op jit(solution)/shard_map/ppermute | solution.py:303
  84.0 0.7 collective-permute-start.12
  84.7 0.0 collective-permute-done.4
  84.7 1.3 %fusion.6 = (bf16[512,256]{1,0:T(8,128)(2,1)S(1)}, bf16[512,256]{1,0:T(8,128)(2,1)S(1)}, bf16[512,256]{1,0:T(8,128)(2,1)S(1)}) fusion(bf16[4,512,256]{2,1,0:T(8,128)(2,1)} %collective-permute-done.4, bf16[4,512,256]{2,1,0:T(8,128)(2,1)S(1)} %keep.1), kind=kLoop, calls=%fused_computation.17 | loop fusion | flops 1572864 | bytes 2359296 | tf_op jit(solution)/shard_map/convert_element_type | solution.py:426
  86.0 6.4 %collective-permute-done.12 = bf16[4,128,128]{2,1,0:T(8,128)(2,1)S(1)} collective-permute-done((bf16[4,128,128]{2,1,0:T(8,128)(2,1)S(1)}, bf16[4,128,128]{2,1,0:T(8,128)(2,1)S(1)}, u32[]{:S(2)}, u32[]{:S(2)}) %collective-permute-start.12) | collective-permute-done | bytes 131104 | tf_op jit(solution)/shard_map/ppermute | solution.py:303
  92.5 0.3 collective-permute-start.13
  92.8 0.0 copy-done.3
  92.8 0.1 broadcast_compare_fusion
  92.9 4.7 %collective-permute-done.13 = bf16[4,128,128]{2,1,0:T(8,128)(2,1)S(1)} collective-permute-done((bf16[4,128,128]{2,1,0:T(8,128)(2,1)S(1)}, bf16[4,128,128]{2,1,0:T(8,128)(2,1)S(1)}, u32[]{:S(2)}, u32[]{:S(2)}) %collective-permute-start.13) | collective-permute-done | bytes 131104 | tf_op jit(solution)/shard_map/ppermute | solution.py:303
  97.6 0.8 select_reduce_fusion
  98.4 4.8 %all-to-all-start.2 = ((bf16[4,128,128]{2,1,0:T(8,128)(2,1)}), bf16[4,128,128]{2,1,0:T(8,128)(2,1)S(1)}, u32[]{:S(2)}, u32[]{:S(2)}) async-start(bf16[4,128,128]{2,1,0:T(8,128)(2,1)} %select_reduce_fusion), calls=%async_computation.2 | async-start | bytes 262144 | tf_op jit(solution)/shard_map/all_to_all | solution.py:309
  103.2 3.0 %collective-permute-start.5 = (bf16[512,256]{1,0:T(8,128)(2,1)S(1)}, bf16[512,256]{1,0:T(8,128)(2,1)S(1)}, u32[]{:S(2)}, u32[]{:S(2)}) collective-permute-start(bf16[512,256]{1,0:T(8,128)(2,1)S(1)} %get-tuple-element.18), channel_id=1, source_target_pairs={{0,4},{1,5},{2,6},{3,7},{4,0},{5,1},{6,2},{7,3},{8,12},{9,13},{10,... | collective-permute-start | bytes 786440 | tf_op jit(solution)/shard_map/ppermute | solution.py:439
  106.2 0.6 collective-permute-start.6
  106.8 2.7 %collective-permute-start.7 = (bf16[512,256]{1,0:T(8,128)(2,1)S(1)}, bf16[512,256]{1,0:T(8,128)(2,1)S(1)}, u32[]{:S(2)}, u32[]{:S(2)}) collective-permute-start(bf16[512,256]{1,0:T(8,128)(2,1)S(1)} %get-tuple-element.19), channel_id=1, source_target_pairs={{0,6},{1,7},{2,0},{3,1},{4,2},{5,3},{6,4},{7,5},{8,14},{9,15},{10,... | collective-permute-start | bytes 786440 | tf_op jit(solution)/shard_map/ppermute | solution.py:439
  109.4 0.0 all-to-all-done.2
  109.4 0.7 bitcast_convert_fusion
  110.2 2.6 %collective-permute-done.5 = bf16[512,256]{1,0:T(8,128)(2,1)S(1)} collective-permute-done((bf16[512,256]{1,0:T(8,128)(2,1)S(1)}, bf16[512,256]{1,0:T(8,128)(2,1)S(1)}, u32[]{:S(2)}, u32[]{:S(2)}) %collective-permute-start.5) | collective-permute-done | bytes 262176 | tf_op jit(solution)/shard_map/ppermute | solution.py:439
  112.7 2.7 %collective-permute-done.6 = bf16[512,256]{1,0:T(8,128)(2,1)S(1)} collective-permute-done((bf16[512,256]{1,0:T(8,128)(2,1)S(1)}, bf16[512,256]{1,0:T(8,128)(2,1)S(1)}, u32[]{:S(2)}, u32[]{:S(2)}) %collective-permute-start.6) | collective-permute-done | bytes 262176 | tf_op jit(solution)/shard_map/ppermute | solution.py:439
  115.4 0.1 collective-permute-done.7
  115.5 1.8 %fusion.5 = bf16[512,256]{1,0:T(8,128)(2,1)} fusion(bf16[512,256]{1,0:T(8,128)(2,1)S(1)} %collective-permute-done.7, bf16[512,256]{1,0:T(8,128)(2,1)S(1)} %collective-permute-done.6, bf16[512,256]{1,0:T(8,128)(2,1)S(1)} %collective-permute-done.5, bf16[4,512,256]{2,1,0:T(8,128)(2,1)} %collective-permute-done.4, bf16[4,512,256]{2,1,0:T(8,128)(2,1)S(1)} %keep.1), kind=kLoop, calls=%fused_computation.12 | loop fusion | flops 1310720 | bytes 1572864 | tf_op jit(solution)/shard_map/convert_element_type | solution.py:446
  (8 shorter events, 0.2 us)
Async XLA Ops:
  15.7 12.9 %all-to-all-start = ((bf16[4,2,128,128]{3,2,1,0:T(8,128)(2,1)}), bf16[4,2,128,128]{3,2,1,0:T(8,128)(2,1)S(1)}, u32[]{:S(2)}, u32[]{:S(2)}) async-start(bf16[4,2,128,128]{3,2,1,0:T(8,128)(2,1)} %get-tuple-element.12), calls=%async_computation | async-start | bytes 524288 | tf_op jit(solution)/shard_map/all_to_all | solution.py:309
  23.1 36.1 %copy-start = (f32[4,512,128]{2,1,0:T(8,128)S(1)}, f32[4,512,128]{2,1,0:T(8,128)}, u32[]{:S(2)}) copy-start(f32[4,512,128]{2,1,0:T(8,128)} %get-tuple-element.10.out_ref) | copy-start | bytes 3145732
  23.1 36.1 %copy-start.1 = (bf16[4,512,128]{2,1,0:T(8,128)(2,1)S(1)}, bf16[4,512,128]{2,1,0:T(8,128)(2,1)}, u32[]{:S(2)}) copy-start(bf16[4,512,128]{2,1,0:T(8,128)(2,1)} %get-tuple-element.11.link_ref) | copy-start | bytes 1572868
  23.1 36.1 %copy-start.2 = (f32[128]{0:T(128)S(1)}, f32[128]{0:T(128)}, u32[]{:S(2)}) copy-start(f32[128]{0:T(128)} %param.16) | copy-start | bytes 1540
  23.1 38.9 %collective-permute-start.10 = (bf16[5,128,128]{2,1,0:T(8,128)(2,1)}, bf16[5,128,128]{2,1,0:T(8,128)(2,1)}, u32[]{:S(2)}, u32[]{:S(2)}) collective-permute-start(bf16[5,128,128]{2,1,0:T(8,128)(2,1)} %get-tuple-element.22), channel_id=1, source_target_pairs={{0,8},{8,16},{16,24},{24,0},{32,40},{40,48},{48,56},{56,32},{64,72... | collective-permute-start | bytes 491528 | tf_op jit(solution)/shard_map/ppermute | solution.py:368
  24.7 38.2 %collective-permute-start.9 = (bf16[5,128,128]{2,1,0:T(8,128)(2,1)}, bf16[5,128,128]{2,1,0:T(8,128)(2,1)}, u32[]{:S(2)}, u32[]{:S(2)}) collective-permute-start(bf16[5,128,128]{2,1,0:T(8,128)(2,1)} %get-tuple-element.23), channel_id=1, source_target_pairs={{0,16},{8,24},{16,0},{24,8},{32,48},{40,56},{48,32},{56,40},{64,80... | collective-permute-start | bytes 491528 | tf_op jit(solution)/shard_map/ppermute | solution.py:368
  25.4 38.4 %collective-permute-start.8 = (bf16[5,128,128]{2,1,0:T(8,128)(2,1)}, bf16[5,128,128]{2,1,0:T(8,128)(2,1)}, u32[]{:S(2)}, u32[]{:S(2)}) collective-permute-start(bf16[5,128,128]{2,1,0:T(8,128)(2,1)} %get-tuple-element.21), channel_id=1, source_target_pairs={{0,24},{8,0},{16,8},{24,16},{32,56},{40,32},{48,40},{56,48},{64,88... | collective-permute-start | bytes 491528 | tf_op jit(solution)/shard_map/ppermute | solution.py:368
  29.1 15.3 %collective-permute-start.2 = (bf16[128,256]{1,0:T(8,128)(2,1)S(1)}, bf16[128,256]{1,0:T(8,128)(2,1)S(1)}, u32[]{:S(2)}, u32[]{:S(2)}) collective-permute-start(bf16[128,256]{1,0:T(8,128)(2,1)S(1)} %fusion.1), channel_id=1, source_target_pairs={{0,96},{8,104},{16,112},{24,120},{32,128},{40,136},{48,144},{56,15... | collective-permute-start | bytes 196616 | tf_op jit(solution)/shard_map/ppermute | solution.py:298
  35.1 8.0 %collective-permute-start.3 = (bf16[128,128]{1,0:T(8,128)(2,1)S(1)}, bf16[128,128]{1,0:T(8,128)(2,1)S(1)}, u32[]{:S(2)}, u32[]{:S(2)}) collective-permute-start(bf16[128,128]{1,0:T(8,128)(2,1)S(1)} %fusion.2), channel_id=1, source_target_pairs={{0,128},{8,136},{16,144},{24,152},{32,160},{40,168},{48,176},{56,1... | collective-permute-start | bytes 98312 | tf_op jit(solution)/shard_map/ppermute | solution.py:298
  43.1 3.9 %collective-permute-start = (bf16[128,256]{1,0:T(8,128)(2,1)S(1)}, bf16[128,256]{1,0:T(8,128)(2,1)S(1)}, u32[]{:S(2)}, u32[]{:S(2)}) collective-permute-start(bf16[128,256]{1,0:T(8,128)(2,1)S(1)} %fusion.1), channel_id=1, source_target_pairs={{0,32},{8,40},{16,48},{24,56},{32,64},{40,72},{48,80},{56,88},{64,... | collective-permute-start | bytes 196616 | tf_op jit(solution)/shard_map/ppermute | solution.py:298
  44.4 4.3 %collective-permute-start.1 = (bf16[128,256]{1,0:T(8,128)(2,1)S(1)}, bf16[128,256]{1,0:T(8,128)(2,1)S(1)}, u32[]{:S(2)}, u32[]{:S(2)}) collective-permute-start(bf16[128,256]{1,0:T(8,128)(2,1)S(1)} %fusion.1), channel_id=1, source_target_pairs={{0,64},{8,72},{16,80},{24,88},{32,96},{40,104},{48,112},{56,120},{... | collective-permute-start | bytes 196616 | tf_op jit(solution)/shard_map/ppermute | solution.py:298
  50.0 9.3 %all-to-all-start.1 = ((bf16[4,128,128]{2,1,0:T(8,128)(2,1)}), bf16[4,128,128]{2,1,0:T(8,128)(2,1)S(1)}, u32[]{:S(2)}, u32[]{:S(2)}) async-start(bf16[4,128,128]{2,1,0:T(8,128)(2,1)} %get-tuple-element.32), calls=%async_computation.1 | async-start | bytes 262144 | tf_op jit(solution)/shard_map/all_to_all | solution.py:309
  61.9 22.8 %collective-permute-start.4 = (bf16[4,512,256]{2,1,0:T(8,128)(2,1)S(1)}, bf16[4,512,256]{2,1,0:T(8,128)(2,1)}, u32[]{:S(2)}, u32[]{:S(2)}) collective-permute-start(bf16[4,512,256]{2,1,0:T(8,128)(2,1)S(1)} %get-tuple-element.14), channel_id=1, source_target_pairs={{0,1},{1,0},{2,3},{3,2},{4,5},{5,4},{6,7},{7,6},{8,9},{9,8},{10,11... | collective-permute-start | bytes 3145736 | tf_op jit(solution)/shard_map/ppermute | solution.py:416
  66.0 18.0 %collective-permute-start.11 = (bf16[4,128,128]{2,1,0:T(8,128)(2,1)S(1)}, bf16[4,128,128]{2,1,0:T(8,128)(2,1)S(1)}, u32[]{:S(2)}, u32[]{:S(2)}) collective-permute-start(bf16[4,128,128]{2,1,0:T(8,128)(2,1)S(1)} %fusion.12), channel_id=1, source_target_pairs={{0,128},{8,136},{16,144},{24,152},{32,160},{40,168},{48,176},{56,1... | collective-permute-start | bytes 393224 | tf_op jit(solution)/shard_map/ppermute | solution.py:303
  79.3 13.5 %copy-start.3 = (s32[4]{0:T(128)S(1)}, s32[4]{0:T(128)}, u32[]{:S(2)}) copy-start(s32[4]{0:T(128)} %param.15) | copy-start | bytes 52
  84.0 8.4 %collective-permute-start.12 = (bf16[4,128,128]{2,1,0:T(8,128)(2,1)S(1)}, bf16[4,128,128]{2,1,0:T(8,128)(2,1)S(1)}, u32[]{:S(2)}, u32[]{:S(2)}) collective-permute-start(bf16[4,128,128]{2,1,0:T(8,128)(2,1)S(1)} %add.132), channel_id=1, source_target_pairs={{0,64},{8,72},{16,80},{24,88},{32,96},{40,104},{48,112},{56,120},{... | collective-permute-start | bytes 393224 | tf_op jit(solution)/shard_map/ppermute | solution.py:303
  92.5 5.1 %collective-permute-start.13 = (bf16[4,128,128]{2,1,0:T(8,128)(2,1)S(1)}, bf16[4,128,128]{2,1,0:T(8,128)(2,1)S(1)}, u32[]{:S(2)}, u32[]{:S(2)}) collective-permute-start(bf16[4,128,128]{2,1,0:T(8,128)(2,1)S(1)} %add.133), channel_id=1, source_target_pairs={{0,32},{8,40},{16,48},{24,56},{32,0},{40,8},{48,16},{56,24},{64,96... | collective-permute-start | bytes 393224 | tf_op jit(solution)/shard_map/ppermute | solution.py:303
  98.4 11.0 %all-to-all-start.2 = ((bf16[4,128,128]{2,1,0:T(8,128)(2,1)}), bf16[4,128,128]{2,1,0:T(8,128)(2,1)S(1)}, u32[]{:S(2)}, u32[]{:S(2)}) async-start(bf16[4,128,128]{2,1,0:T(8,128)(2,1)} %select_reduce_fusion), calls=%async_computation.2 | async-start | bytes 262144 | tf_op jit(solution)/shard_map/all_to_all | solution.py:309
  103.2 9.6 %collective-permute-start.5 = (bf16[512,256]{1,0:T(8,128)(2,1)S(1)}, bf16[512,256]{1,0:T(8,128)(2,1)S(1)}, u32[]{:S(2)}, u32[]{:S(2)}) collective-permute-start(bf16[512,256]{1,0:T(8,128)(2,1)S(1)} %get-tuple-element.18), channel_id=1, source_target_pairs={{0,4},{1,5},{2,6},{3,7},{4,0},{5,1},{6,2},{7,3},{8,12},{9,13},{10,... | collective-permute-start | bytes 786440 | tf_op jit(solution)/shard_map/ppermute | solution.py:439
  106.2 9.2 %collective-permute-start.6 = (bf16[512,256]{1,0:T(8,128)(2,1)S(1)}, bf16[512,256]{1,0:T(8,128)(2,1)S(1)}, u32[]{:S(2)}, u32[]{:S(2)}) collective-permute-start(bf16[512,256]{1,0:T(8,128)(2,1)S(1)} %get-tuple-element.20), channel_id=1, source_target_pairs={{0,2},{1,3},{2,4},{3,5},{4,6},{5,7},{6,0},{7,1},{8,10},{9,11},{10,... | collective-permute-start | bytes 786440 | tf_op jit(solution)/shard_map/ppermute | solution.py:439
  106.8 8.8 %collective-permute-start.7 = (bf16[512,256]{1,0:T(8,128)(2,1)S(1)}, bf16[512,256]{1,0:T(8,128)(2,1)S(1)}, u32[]{:S(2)}, u32[]{:S(2)}) collective-permute-start(bf16[512,256]{1,0:T(8,128)(2,1)S(1)} %get-tuple-element.19), channel_id=1, source_target_pairs={{0,6},{1,7},{2,0},{3,1},{4,2},{5,3},{6,4},{7,5},{8,14},{9,15},{10,... | collective-permute-start | bytes 786440 | tf_op jit(solution)/shard_map/ppermute | solution.py:439
